TPU v7x, 32 devices: a whole 2x2x4 slice. The times are simulated.
32 devices in a mesh: gx: 8 (over y, x, core), gy: 4 (over z).
Axes of the slice: x: 2, y: 2, z: 4, core: 2. Of those that a mesh axis runs over, the one named last changes fastest.
Arguments:
- quotient_table: float32 [32768, 256], P(('gx', 'gy')), may hold values from -6 to 6
- quotient_acc: float32 [32768, 256], P(('gx', 'gy')), may hold values from 1 to 64
- remainder_table: float32 [4096, 256], replicated, may hold values from -6 to 6
- remainder_acc: float32 [4096, 256], P(('gx', 'gy')), may hold values from 1 to 64
- cotangent: bfloat16 [2048, 256], P(('gx', 'gy')), may hold values from -6 to 6
- quotient_ids: int32 [2048, 20], P(('gx', 'gy')), may hold values from 0 to 32767, as said below
- remainder_ids: int32 [2048, 20], P(('gx', 'gy')), may hold values from 0 to 4095
Outputs:
- new_quotient: float32 [32768, 256], P(('gx', 'gy'))
- new_quotient_acc: float32 [32768, 256], P(('gx', 'gy'))
- new_remainder: float32 [4096, 256], replicated
- new_remainder_acc: float32 [4096, 256], P(('gx', 'gy'))
Inputs may be any that keep to these rules, and one draw needn't show every extreme that they name: `quotient_ids`: call the rows k * 1024 to (k + 1) * 1024 - 1 the range of device k along gx+gy. Of the ids of one device's 64 samples, at most 80 fall in any one range; in every draw some range receives exactly 80 from every device.
All inputs are finite; a program needn't handle non-finite values.
Results may differ from a plain program's by a relative error of at most 0.0046.
Values may be sent and summed in bfloat16 or wider, within the bound.
A program may use at most 64 MiB of HBM per device.

v0:
```python
import jax
import jax.numpy as jnp
from jax import lax
from jax.sharding import PartitionSpec as P

LEARNING_RATE = 0.1
EPSILON = 1e-10


def adagrad(param, accum, grad):
    fresh = accum + grad * grad
    return (param - LEARNING_RATE * grad / (jnp.sqrt(fresh) + EPSILON), fresh)


def block_sums(ids, values, count):
    block = count
    if count > 1024 and count % 1024 == 0:
        block = 1024

    def one(first):
        wanted = first + jnp.arange(block, dtype=jnp.int32)
        hit = (wanted[:, None] == ids[None, :]).astype(jnp.bfloat16)
        return jnp.dot(hit, values, preferred_element_type=jnp.float32)

    firsts = jnp.arange(count // block, dtype=jnp.int32) * block
    return lax.map(one, firsts).reshape(count, values.shape[1])


def local(
    quotient_table,
    quotient_acc,
    remainder_table,
    remainder_acc,
    cotangent,
    quotient_ids,
    remainder_ids,
):
    devices = lax.axis_size(("gx", "gy"))
    q_dev, width = quotient_table.shape
    r_rows = remainder_table.shape[0]
    share = remainder_acc.shape[0]
    samples, bag = quotient_ids.shape
    count = samples * bag
    capacity = max(2, (2 * count + devices - 1) // devices)
    table_slots = devices * capacity
    flat_q = quotient_ids.reshape(count)
    flat_r = remainder_ids.reshape(count)
    owner = flat_q // q_dev
    local_row = flat_q - owner * q_dev
    order = jnp.argsort(owner, stable=True)
    sorted_owner = owner[order]
    column = jnp.arange(devices, dtype=jnp.int32)
    tally = jnp.sum((owner[:, None] == column[None, :]).astype(jnp.int32), axis=0)
    begins = jnp.cumsum(tally) - tally
    placed = sorted_owner * capacity + jnp.arange(count, dtype=jnp.int32) - begins[sorted_owner]
    target = jnp.zeros((count,), jnp.int32).at[order].set(placed)
    local_sent = (
        jnp.zeros((table_slots,), jnp.int32).at[target].set(local_row).reshape(devices, capacity)
    )
    cot_rows = jnp.repeat(cotangent, bag, axis=0)
    asked = lax.all_to_all(local_sent, ("gx", "gy"), split_axis=0, concat_axis=0, tiled=True)
    asked_flat = asked.reshape(table_slots)
    found = quotient_table[asked_flat].astype(jnp.bfloat16).reshape(devices, capacity, width)
    replies = lax.all_to_all(found, ("gx", "gy"), split_axis=0, concat_axis=0, tiled=True)
    q_rows = replies.reshape(table_slots, width)[target]
    rem_rows = lax.optimization_barrier(remainder_table[flat_r].astype(jnp.bfloat16))
    cot_wide = cot_rows.astype(jnp.float32)
    q_terms = (cot_wide * rem_rows.astype(jnp.float32)).astype(jnp.bfloat16)
    r_values = (cot_wide * q_rows.astype(jnp.float32)).astype(jnp.bfloat16)
    outgoing = (
        jnp.zeros((table_slots, width), jnp.bfloat16)
        .at[target]
        .set(q_terms)
        .reshape(devices, capacity, width)
    )
    arrived = lax.all_to_all(outgoing, ("gx", "gy"), split_axis=0, concat_axis=0, tiled=True)
    q_values = arrived.reshape(table_slots, width)
    quotient_grad = block_sums(asked_flat, q_values, q_dev)
    new_quotient, new_quotient_acc = adagrad(quotient_table, quotient_acc, quotient_grad)
    first = lax.axis_index(("gx", "gy")) * share
    partial_grad = block_sums(flat_r, r_values, r_rows)
    total = lax.psum(partial_grad, ("gx", "gy"))
    grad_share = lax.dynamic_slice_in_dim(total, first, share, 0)
    param_share = lax.dynamic_slice_in_dim(remainder_table, first, share, 0)
    new_share, new_remainder_acc = adagrad(param_share, remainder_acc, grad_share)
    new_remainder = lax.all_gather(new_share, ("gx", "gy"), axis=0, tiled=True)
    return (new_quotient, new_quotient_acc, new_remainder, new_remainder_acc)


def solution(mesh):
    return jax.shard_map(
        local,
        mesh=mesh,
        in_specs=(
            P(("gx", "gy"), None),
            P(("gx", "gy"), None),
            P(),
            P(("gx", "gy"), None),
            P(("gx", "gy"), None),
            P(("gx", "gy"), None),
            P(("gx", "gy"), None),
        ),
        out_specs=(P(("gx", "gy"), None), P(("gx", "gy"), None), P(), P(("gx", "gy"), None)),
        check_vma=False,
    )
```

profile of v0, /device:TPU:0, one launch (start us, length us, event | category | flops | bytes accessed | tf_op | source)
XLA Modules:
  0.0 350.6 jit_solution(3329541990858526170)
XLA Ops:
  9.9 5.0 %sort.17 = (s32[1280]{0:T(1024)}, s32[1280]{0:T(1024)S(1)}) sort(s32[1280]{0:T(1024)S(1)} %get-tuple-element.98, s32[1280]{0:T(1024)S(1)} %iota.24), dimensions={0}, to_apply=%region_0.1 | sort | flops 14080 | bytes 20480 | tf_op jit(solution)/shard_map/jit(argsort)/sort | solution.py:50
  15.0 7.1 %gather_fusion = s32[1280]{0:T(1024)S(1)} fusion(s32[1280]{0:T(1024)S(1)} %get-tuple-element.98, s32[2048]{0:T(1024)S(1)} %pad_clamp_fusion.3), kind=kCustom, calls=%fused_computation | custom fusion | bytes 15360 | tf_op jit(solution)/shard_map/gather | solution.py:51
  22.1 4.3 %fusion.19 = (s32[1280]{0:T(1024)S(1)}, s32[1280,1]{0,1:T(1,128)S(1)}) fusion(s32[]{:T(128)} %bitcast.28, s32[]{:T(128)} %bitcast.29, s32[]{:T(128)} %bitcast.30, s32[]{:T(128)} %bitcast.31, s32[]{:T(128)} %bitcast.32, s32[]{:T(128)} %bitcast.34, s32[]{:T(128)} %bitcast.33, s32[1280]{0:T(1024)S(1)} %gather_fusion), kind=kLoop, calls=%fused_computation.79 | loop fusion | flops 19200 | bytes 15388 | tf_op jit(solution)/shard_map/gather | solution.py:55
  26.8 15.8 %select_subtract_fusion = s32[1280]{0:T(1024)S(1)} fusion(pred[1280]{0:T(1024)(128)(4,1)S(1)} %get-tuple-element.80, pred[1280]{0:T(1024)(128)(4,1)S(1)} %get-tuple-element.79, pred[1280]{0:T(1024)(128)(4,1)S(1)} %get-tuple-element.78, pred[1280]{0:T(1024)(128)(4,1)S(1)} %get-tuple-element.77, pred[1280]{0:T(1024)(128)(4,1)S(1)} %get-tuple-element.76, ...), kind=kLoop, calls=%fused_computation.73 | loop fusion | flops 35840 | bytes 47460 | tf_op jit(solution)/shard_map/sub | solution.py:55
  42.6 5.2 %scatter_custom_fusion = s32[1280]{0:T(1024)S(1)} fusion(s32[1280]{0:T(1024)S(1)} %compare_select_fusion.4, s32[1280]{0:T(1024)S(1)} %select_subtract_fusion, s32[]{:T(128)} %constant.26.clone.1), kind=kCustom, calls=%fused_computation.81 | custom fusion | bytes 5124 | tf_op jit(solution)/shard_map/scatter | solution.py:56
  47.8 5.3 %scatter_custom_fusion.1 = s32[2560]{0:T(1024)S(1)} fusion(s32[1280]{0:T(1024)S(1)} %compare_select_fusion.3, s32[1280]{0:T(1024)S(1)} %get-tuple-element.97, s32[]{:T(128)} %constant.26.clone.1), kind=kCustom, calls=%fused_computation.77 | custom fusion | bytes 10244 | tf_op jit(solution)/shard_map/scatter | solution.py:58
  53.2 14.3 %all_to_all.19 = s32[32,1,80]{2,1,0:T(1,128)S(1)} all-to-all(s32[32,1,80]{2,1,0:T(1,128)S(1)} %all_to_all.12), channel_id=1, replica_groups=mesh['gx'=8,'gy'=4] {'gx','gy'}, dimensions={0} | all-to-all | bytes 20480 | tf_op jit(solution)/shard_map/all_to_all | solution.py:61
  67.7 6.8 %gather_fusion.2 = bf16[2560,256]{1,0:T(8,128)(2,1)} fusion(f32[1024,256]{1,0:T(8,128)S(1)} %copy-done, s32[3072]{0:T(1024)S(1)} %pad_clamp_fusion), kind=kCustom, calls=%fused_computation.2 | custom fusion | bytes 2631680 | tf_op jit(solution)/shard_map/gather | solution.py:63
  74.5 2.8 all-to-all-start.2
  78.6 2.5 convert_element_type.37
  81.3 26.4 %all-to-all-done.2 = bf16[32,80,256]{2,1,0:T(8,128)(2,1)S(1)} async-done(((bf16[32,80,256]{2,1,0:T(8,128)(2,1)}), bf16[32,80,256]{2,1,0:T(8,128)(2,1)S(1)}, u32[]{:S(2)}, u32[]{:S(2)}) %all-to-all-start.2) | async-done | bytes 1310752 | tf_op jit(solution)/shard_map/all_to_all | solution.py:64
  107.6 4.1 %gather_fusion.3 = bf16[1280,256]{1,0:T(8,128)(2,1)S(1)} fusion(bf16[2560,256]{1,0:T(8,128)(2,1)S(1)} %bitcast.55, s32[2048]{0:T(1024)S(1)} %pad_clamp_fusion.1), kind=kCustom, calls=%fused_computation.3 | custom fusion | bytes 1315840 | tf_op jit(solution)/shard_map/gather | solution.py:65
  113.2 12.5 %while.3 = (s32[]{:T(128)}, f32[4,1024,256]{2,1,0:T(8,128)}, s32[4]{0:T(128)S(1)}, s32[64,20]{1,0:T(8,128)}, bf16[1280,256]{1,0:T(8,128)(2,1)S(1)}, /*index=5*/s32[1280]{0:T(1024)S(1)}, s32[]{:T(128)}) while((s32[]{:T(128)}, f32[4,1024,256]{2,1,0:T(8,128)}, s32[4]{0:T(128)S(1)}, s32[64,20]{1,0:T(8,128)}, ...), condition=%wide.wide.region_7.8_spmd, body=%wide.wide.region_6.7_spmd.sunk | while | flops 672400384 | bytes 1717853 | solution.py:26
  117.5 1.9 fusion.35
  120.7 1.9 fusion.35
  123.8 1.9 fusion.35
  125.8 142.5 %all-reduce.2.cloned.1.call-done = f32[4096,256]{1,0:T(8,128)} async-done(((f32[4096,256]{1,0:T(8,128)}), f32[4096,256]{1,0:T(8,128)}) %all-reduce.2.cloned.1.call-update) | async-done | bytes 4194320 | tf_op jit(solution)/shard_map/psum | solution.py:82
  270.2 5.4 %gather_fusion.1 = bf16[1280,256]{1,0:T(8,128)(2,1)S(1)} fusion(f32[4096,256]{1,0:T(8,128)} %param.11, s32[2048]{0:T(1024)S(1)} %pad_clamp_fusion.2), kind=kCustom, calls=%fused_computation.1 | custom fusion | bytes 1315840 | tf_op jit(solution)/shard_map/gather | solution.py:66
  275.6 9.3 %scatter_custom_fusion.2 = bf16[2560,256]{1,0:T(8,128)(2,1)} fusion(s32[1280]{0:T(1024)S(1)} %compare_select_fusion.3, f32[1280,256]{1,0:T(8,128)S(1)} %copy-done.1, bf16[1280,256]{1,0:T(8,128)(2,1)S(1)} %gather_fusion.1, bf16[]{:T(256)} %constant.39.clone.1), kind=kCustom, calls=%fused_computation.21 | custom fusion | flops 983040 | bytes 3276802 | tf_op jit(solution)/shard_map/scatter | solution.py:73
  284.9 3.9 %all-to-all-start.1 = ((bf16[32,80,256]{2,1,0:T(8,128)(2,1)}), bf16[32,80,256]{2,1,0:T(8,128)(2,1)S(1)}, u32[]{:S(2)}, u32[]{:S(2)}) async-start(bf16[32,80,256]{2,1,0:T(8,128)(2,1)} %bitcast.57), calls=%async_computation.1 | async-start | bytes 2621440 | tf_op jit(solution)/shard_map/all_to_all | solution.py:76
  290.1 39.1 %all-to-all-done.1 = bf16[32,80,256]{2,1,0:T(8,128)(2,1)S(1)} async-done(((bf16[32,80,256]{2,1,0:T(8,128)(2,1)}), bf16[32,80,256]{2,1,0:T(8,128)(2,1)S(1)}, u32[]{:S(2)}, u32[]{:S(2)}) %all-to-all-start.1) | async-done | bytes 1310752 | tf_op jit(solution)/shard_map/all_to_all | solution.py:76
  329.1 4.7 %divide_subtract_fusion = (f32[1024,256]{1,0:T(8,128)}, f32[1024,256]{1,0:T(8,128)}) fusion(f32[1024,256]{1,0:T(8,128)S(1)} %copy-done, f32[1024,256]{1,0:T(8,128)} %param.10, bf16[2560,256]{1,0:T(8,128)(2,1)S(1)} %bitcast.59, s32[2560]{0:T(1024)S(1)} %eq.54), kind=kOutput, calls=%fused_computation.19 | convolution fusion | flops 1346371584 | bytes 5515264 | tf_op jit(solution)/shard_map/while/body/eval_jaxpr/dot_general | solution.py:23
  333.8 5.5 %all-gather.2.cloned.1.call-done = f32[4096,256]{1,0:T(8,128)} async-done(((f32[128,256]{1,0:T(8,128)}), f32[4096,256]{1,0:T(8,128)}) %all-gather.2.cloned.1.call-update) | async-done | bytes 4194320 | tf_op jit(solution)/shard_map/all_gather | solution.py:86
  339.3 4.5 %copy.29 = f32[4096,256]{1,0:T(8,128)} copy(f32[4096,256]{1,0:T(8,128)} %all-gather.2.cloned.1.call-done) | data formatting | bytes 8388608
  (60 shorter events, 16.4 us)
Async XLA Ops:
  15.0 52.7 %copy-start = (f32[1024,256]{1,0:T(8,128)S(1)}, f32[1024,256]{1,0:T(8,128)}, u32[]{:S(2)}) copy-start(f32[1024,256]{1,0:T(8,128)} %param.9) | copy-start | bytes 3145732
  74.5 2.9 copy-start.5
  74.5 33.2 %all-to-all-start.2 = ((bf16[32,80,256]{2,1,0:T(8,128)(2,1)}), bf16[32,80,256]{2,1,0:T(8,128)(2,1)S(1)}, u32[]{:S(2)}, u32[]{:S(2)}) async-start(bf16[32,80,256]{2,1,0:T(8,128)(2,1)} %bitcast.56), calls=%async_computation.2 | async-start | bytes 2621440 | tf_op jit(solution)/shard_map/all_to_all | solution.py:64
  77.3 191.0 %all-reduce.2.cloned.1.call-start = ((), (), s32[]{:S(2)}) async-start(), calls=%async_computation.3 | async-start | bytes 8388608 | tf_op jit(solution)/shard_map/psum | solution.py:82
  78.6 2.5 copy-start.6
  81.1 30.6 %copy-start.2 = (s32[64,20]{1,0:T(8,128)}, s32[64,20]{1,0:T(8,128)S(1)}, u32[]{:S(2)}) copy-start(s32[64,20]{1,0:T(8,128)S(1)} %copy.18) | copy-start | bytes 15364
  125.7 142.6 %copy-start.4 = (f32[128,256]{1,0:T(8,128)S(1)}, f32[128,256]{1,0:T(8,128)}, u32[]{:S(2)}) copy-start(f32[128,256]{1,0:T(8,128)} %param.12) | copy-start | bytes 393220
  125.7 144.3 %copy-start.3 = (s32[64,20]{1,0:T(8,128)S(1)}, s32[64,20]{1,0:T(8,128)}, u32[]{:S(2)}) copy-start(s32[64,20]{1,0:T(8,128)} %get-tuple-element.230) | copy-start | bytes 15364
  125.7 213.6 %all-gather.2.cloned.1.call-start = ((), (), s32[]{:S(2)}) async-start(), calls=%async_computation.4 | async-start | bytes 4325376 | tf_op jit(solution)/shard_map/all_gather | solution.py:86
  270.2 5.4 %copy-start.1 = (f32[1280,256]{1,0:T(8,128)S(1)}, f32[1280,256]{1,0:T(8,128)}, u32[]{:S(2)}) copy-start(f32[1280,256]{1,0:T(8,128)} %convert_element_type.37) | copy-start | bytes 3932164
  284.9 44.2 %all-to-all-start.1 = ((bf16[32,80,256]{2,1,0:T(8,128)(2,1)}), bf16[32,80,256]{2,1,0:T(8,128)(2,1)S(1)}, u32[]{:S(2)}, u32[]{:S(2)}) async-start(bf16[32,80,256]{2,1,0:T(8,128)(2,1)} %bitcast.57), calls=%async_computation.1 | async-start | bytes 2621440 | tf_op jit(solution)/shard_map/all_to_all | solution.py:76
Sparse Core Ops, SparseCore 0:
  125.8 142.3 all-reduce.1
  271.3 68.0 all-gather.1
where the time goes:
time: 352 us; the launch traced here: 351 us
  waiting for transfers between devices  213 us (61%)
  local copies, waits for them, and re-layouts  47.9 us (14%)
  other arithmetic  41.6 us (12%)
  blocking collectives  14.3 us (4%)
  between operations  14.3 us (4%)
  matrix products  12.2 us (3%)
  starting transfers between devices  6.77 us (2%)
    psum x1, waiting for transfers between devices, local(): total = lax.psum(partial_grad, ('gx', 'gy'))  142 us
    all_to_all x1, waiting for transfers between devices, local(): lax.all_to_all(outgoing, ('gx', 'gy'), split_axis=0, concat_axis=0, tiled...  39.1 us
    all_to_all x1, waiting for transfers between devices, local(): lax.all_to_all(found, ('gx', 'gy'), split_axis=0, concat_axis=0, tiled=True)  26.4 us
    sub x1, other arithmetic, local(): sorted_owner * capacity + jnp.arange(count, dtype=jnp.int32)  15.8 us
    all_to_all x1, blocking collectives, local(): lax.all_to_all(local_sent, ('gx', 'gy'), split_axis=0, concat_axis=0, til...  14.3 us
    dot_general x5, matrix products, one(): return jnp.dot(hit, values, preferred_element_type=jnp.float32)  12.2 us
    scatter x1, other arithmetic, local(): outgoing = jnp.zeros((table_slots, width), jnp.bfloat16).at[target].set(q...  9.26 us
    gather x1, local copies, waits for them, and re-layouts, local(): sorted_owner = owner[order]  7.08 us
  transfers between devices with their start and end apart: 4, of which 4 were waited for; matrix products, arithmetic and copies ran while one was open for 7% of the time, Pallas kernels for 0%

commit v1 on v0

v1 whole, which is shorter than its diff:
```python
import functools

import jax
import jax.numpy as jnp
from jax import lax
from jax.experimental import pallas as pl
from jax.experimental.pallas import tpu as pltpu
from jax.sharding import PartitionSpec as P

LEARNING_RATE = 0.1
EPSILON = 1e-10
MESH = pl.DeviceIdType.MESH
VMEM = pltpu.VMEM


def adagrad(param, accum, grad):
    fresh = accum + grad * grad
    return (param - LEARNING_RATE * grad / (jnp.sqrt(fresh) + EPSILON), fresh)


def weights(size):
    out, w = [], 1
    while w < size:
        out.append(w)
        w *= 2
    return out


class Cube:
    def __init__(self, nx, ny, split):
        gx = [("gx", w, w * ny) for w in weights(nx)]
        gy = [("gy", w, w) for w in reversed(weights(ny))]
        self.orders = [gx + gy]
        if split:
            self.orders.append(gx[:1] + gx[:0:-1] + gy)
        self.bits = len(gx) + len(gy)

    def locate(self):
        self.at = {"gx": lax.axis_index("gx"), "gy": lax.axis_index("gy")}

    def bit(self, entry):
        return (self.at[entry[0]] // entry[1]) % 2

    def partner(self, entry):
        where = dict(self.at)
        where[entry[0]] = where[entry[0]] + entry[1] * (1 - 2 * self.bit(entry))
        return (where["gx"], where["gy"])

    def greet(self):
        barrier = pltpu.get_barrier_semaphore()
        for entry in self.orders[0]:
            pl.semaphore_signal(
                barrier, inc=1, device_id=self.partner(entry), device_id_type=MESH
            )
        pl.semaphore_wait(barrier, self.bits)

    def count(self, stage):
        return 2 ** (self.bits - 1 - stage)

    def base(self, order, stage, flip):
        total = 0
        for t in range(stage + 1):
            b = self.bit(order[t])
            if flip and t == stage:
                b = 1 - b
            total = total + b * order[t][2]
        return total

    def spread(self, order, stage, i):
        free = order[stage + 1 :]
        total = 0
        for t, entry in enumerate(free):
            total += ((i >> (len(free) - 1 - t)) & 1) * entry[2]
        return total


def spread_out(cube, streams, send_sems, recv_sems):
    def copies(k, stage, flip):
        order = cube.orders[k]
        base = cube.base(order, stage, flip)
        n = cube.count(stage)
        out = []
        for i in range(n):
            block = base + cube.spread(order, stage, i)
            for m, view in enumerate(streams[k]):
                ref = view(block)
                out.append(
                    pltpu.make_async_remote_copy(
                        src_ref=ref,
                        dst_ref=ref,
                        send_sem=send_sems.at[k, m, n - 1 + i],
                        recv_sem=recv_sems.at[k, m, n - 1 + i],
                        device_id=cube.partner(order[stage]),
                        device_id_type=MESH,
                    )
                )
        return out

    for stage in range(cube.bits - 1, -1, -1):
        for k in range(len(streams)):
            if stage < cube.bits - 1:
                for c in copies(k, stage + 1, True):
                    c.wait_recv()
            for c in copies(k, stage, False):
                c.start()
    for k in range(len(streams)):
        for c in copies(k, 0, True):
            c.wait_recv()
        for stage in range(cube.bits):
            for c in copies(k, stage, False):
                c.wait_send()


def gather_kernel(cube, cot, q, r, cots, qs, rs, send_sems, recv_sems, own_sems):
    cube.locate()
    ny = lax.axis_size("gy")
    me = cube.at["gx"] * ny + cube.at["gy"]
    own = [
        pltpu.make_async_copy(src, dst.at[me], own_sems.at[m])
        for m, (src, dst) in enumerate(((cot, cots), (q, qs), (r, rs)))
    ]
    for c in own:
        c.start()
    cube.greet()
    for c in own:
        c.wait()
    half = cot.shape[0] // 2
    streams = [
        [lambda b: cots.at[b, pl.ds(0, half)], lambda b: qs.at[b]],
        [lambda b: cots.at[b, pl.ds(half, half)], lambda b: rs.at[b]],
    ]
    spread_out(cube, streams, send_sems, recv_sems)


def gather_all(nx, ny, cot, q, r):
    devices = nx * ny
    cube = Cube(nx, ny, True)
    vm = pl.BlockSpec(memory_space=VMEM)
    outs = [jax.ShapeDtypeStruct((devices,) + x.shape, x.dtype) for x in (cot, q, r)]
    return pl.pallas_call(
        functools.partial(gather_kernel, cube),
        out_shape=outs,
        in_specs=[vm] * 3,
        out_specs=[vm] * 3,
        scratch_shapes=[
            pltpu.SemaphoreType.DMA((2, 2, devices - 1)),
            pltpu.SemaphoreType.DMA((2, 2, devices - 1)),
            pltpu.SemaphoreType.DMA((3,)),
        ],
        compiler_params=pltpu.CompilerParams(collective_id=0, has_side_effects=True),
        name="gather_all",
    )(cot, q, r)


def reduce_kernel(
    cube, part, acc, fresh, update, held, sent, landed, send_sems, recv_sems, ag_send, ag_recv
):
    cube.locate()
    ny = lax.axis_size("gy")
    me = cube.at["gx"] * ny + cube.at["gy"]
    streams = len(cube.orders)
    rows = part.shape[1] // streams
    cube.greet()

    def copy(k, stage, i, src):
        slot = cube.count(stage) - 1 + i
        return pltpu.make_async_remote_copy(
            src_ref=src,
            dst_ref=landed.at[slot, pl.ds(k * rows, rows)],
            send_sem=send_sems.at[k, slot],
            recv_sem=recv_sems.at[k, slot],
            device_id=cube.partner(cube.orders[k][stage]),
            device_id_type=MESH,
        )

    def source(k, stage, i):
        if stage == 0:
            order = cube.orders[k]
            block = cube.base(order, 0, True) + cube.spread(order, 0, i)
            return part.at[block, pl.ds(k * rows, rows)]
        return sent.at[cube.count(stage) - 1 + i, pl.ds(k * rows, rows)]

    def total(k, stage, i):
        n = cube.count(stage)
        order = cube.orders[k]
        got = landed[n - 1 + i, pl.ds(k * rows, rows), :].astype(jnp.float32)
        if stage == 0:
            block = cube.base(order, 0, False) + i
            mine = part[block, pl.ds(k * rows, rows), :].astype(jnp.float32)
        else:
            mine = held[n - 1 + i, pl.ds(k * rows, rows), :]
        return mine + got

    def stage0_total(k, b, low):
        order = cube.orders[k]
        n = cube.count(0)
        half = n // 2
        got = landed[n - 1 + b * half + low, pl.ds(k * rows, rows), :]
        block = cube.base(order, 0, False) + b * order[1][2] + cube.spread(order, 1, low)
        mine = part[block, pl.ds(k * rows, rows), :]
        return mine.astype(jnp.float32) + got.astype(jnp.float32)

    for k in range(streams):
        for i in range(cube.count(0)):
            copy(k, 0, i, source(k, 0, i)).start()
    for stage in range(1, cube.bits):
        n = cube.count(stage)
        for k in range(streams):
            for i in range(2 * n):
                copy(k, stage - 1, i, source(k, stage - 1, i)).wait_recv()
            b = cube.bit(cube.orders[k][stage])

            def value(side, i, k=k, stage=stage, n=n):
                if stage == 1:
                    return stage0_total(k, side, i)
                return total(k, stage - 1, side * n + i)

            for i in range(n):
                sent[n - 1 + i, pl.ds(k * rows, rows), :] = value(1 - b, i).astype(sent.dtype)
                copy(k, stage, i, source(k, stage, i)).start()
            for i in range(n):
                held[n - 1 + i, pl.ds(k * rows, rows), :] = value(b, i)
    last = cube.bits - 1
    for k in range(streams):
        copy(k, last, 0, source(k, last, 0)).wait_recv()
        grad = total(k, last, 0)
        mine = pl.ds(k * rows, rows)
        new = acc[mine, :] + grad * grad
        fresh[mine, :] = new
        step = LEARNING_RATE * grad / (jnp.sqrt(new) + EPSILON)
        update[me, mine, :] = step.astype(update.dtype)
    views = [
        [lambda b, k=k: update.at[b, pl.ds(k * rows, rows)]] for k in range(streams)
    ]
    spread_out(cube, views, ag_send, ag_recv)
    for k in range(streams):
        for stage in range(cube.bits):
            for i in range(cube.count(stage)):
                copy(k, stage, i, source(k, stage, i)).wait_send()


def reduce_update(nx, ny, part, acc):
    devices = nx * ny
    share, width = acc.shape
    cube = Cube(nx, ny, share % 32 == 0)
    k = len(cube.orders)
    vm = pl.BlockSpec(memory_space=VMEM)
    return pl.pallas_call(
        functools.partial(reduce_kernel, cube),
        out_shape=[
            jax.ShapeDtypeStruct(acc.shape, jnp.float32),
            jax.ShapeDtypeStruct(part.shape, jnp.bfloat16),
        ],
        in_specs=[vm] * 2,
        out_specs=[vm] * 2,
        scratch_shapes=[
            pltpu.VMEM((devices // 2, share, width), jnp.float32),
            pltpu.VMEM((devices // 2, share, width), jnp.bfloat16),
            pltpu.VMEM((devices - 1, share, width), jnp.bfloat16),
            pltpu.SemaphoreType.DMA((k, devices - 1)),
            pltpu.SemaphoreType.DMA((k, devices - 1)),
            pltpu.SemaphoreType.DMA((k, 1, devices - 1)),
            pltpu.SemaphoreType.DMA((k, 1, devices - 1)),
        ],
        compiler_params=pltpu.CompilerParams(
            collective_id=1, has_side_effects=True, vmem_limit_bytes=48 * 2**20
        ),
        name="reduce_update",
    )(part, acc)


def match(ids, wanted):
    return (wanted[:, None] == ids[None, :]).astype(jnp.bfloat16)


def local(
    quotient_table,
    quotient_acc,
    remainder_table,
    remainder_acc,
    cotangent,
    quotient_ids,
    remainder_ids,
    nx,
    ny,
):
    devices = nx * ny
    q_dev, width = quotient_table.shape
    r_rows = remainder_table.shape[0]
    share = remainder_acc.shape[0]
    samples, bag = quotient_ids.shape
    count = samples * bag
    capacity = max(2, (2 * count + devices - 1) // devices)
    slots = devices * capacity
    f32, bf16 = jnp.float32, jnp.bfloat16
    me = lax.axis_index(("gx", "gy"))
    cots, qs, rs = gather_all(
        nx, ny, cotangent, quotient_ids.reshape(1, count), remainder_ids.reshape(1, count)
    )
    qs = qs.reshape(devices, count)
    rs = rs.reshape(devices, count)
    near = qs - me * q_dev
    mine = (near >= 0) & (near < q_dev)
    steps = jnp.arange(count, dtype=jnp.int32)
    before = (steps[:, None] < steps[None, :]).astype(bf16)
    place = jnp.dot(mine.astype(bf16), before, preferred_element_type=f32)
    place = jnp.where(mine, place, -1.0).astype(jnp.int32)
    seat = jnp.arange(capacity, dtype=jnp.int32)
    pick = (place[:, None, :] == seat[None, :, None]).astype(bf16)
    near = jnp.where(mine, near, 0)
    sample = jnp.broadcast_to(steps // bag + 1, (devices, count))
    facts = jnp.stack(
        [near // 256, near % 256, rs // 256, rs % 256, sample // 128, sample % 128], axis=1
    ).astype(bf16)
    told = jnp.einsum("nvk,nck->vnc", facts, pick, preferred_element_type=f32).astype(jnp.int32)
    row = (told[0] * 256 + told[1]).reshape(slots)
    rem = (told[2] * 256 + told[3]).reshape(slots)
    who = told[4] * 128 + told[5]
    whose = (who[:, :, None] == 1 + jnp.arange(samples, dtype=jnp.int32)).astype(bf16)
    cot_rows = jnp.einsum("ncs,nsw->ncw", whose, cots, preferred_element_type=f32)
    cot_rows = cot_rows.reshape(slots, width)
    rem_rows = lax.optimization_barrier(remainder_table[rem].astype(bf16))
    wanted = jnp.arange(q_dev, dtype=jnp.int32)
    q_rows = jnp.dot(
        (row[:, None] == wanted[None, :]).astype(bf16),
        quotient_table.astype(bf16),
        preferred_element_type=f32,
    )
    q_terms = (cot_rows * rem_rows.astype(f32)).astype(bf16)
    r_terms = (cot_rows * q_rows).astype(bf16)
    part = jnp.dot(
        match(rem, jnp.arange(r_rows, dtype=jnp.int32)), r_terms, preferred_element_type=f32
    ).astype(bf16)
    new_remainder_acc, update = reduce_update(
        nx, ny, part.reshape(devices, share, width), remainder_acc
    )
    quotient_grad = jnp.dot(match(row, wanted), q_terms, preferred_element_type=f32)
    new_quotient, new_quotient_acc = adagrad(quotient_table, quotient_acc, quotient_grad)
    new_remainder = remainder_table - update.reshape(r_rows, width).astype(f32)
    return (new_quotient, new_quotient_acc, new_remainder, new_remainder_acc)


def solution(mesh):
    rows = P(("gx", "gy"), None)
    return jax.shard_map(
        functools.partial(local, nx=mesh.shape["gx"], ny=mesh.shape["gy"]),
        mesh=mesh,
        in_specs=(rows, rows, P(), rows, rows, rows, rows),
        out_specs=(rows, rows, P(), rows),
        check_vma=False,
    )
```

time: 352 us -> 125 us (0.36)
  waiting for transfers between devices: 213 us -> 0 us
  Pallas kernels: 0 us -> 72.9 us
  other arithmetic: 41.6 us -> 9.33 us
  local copies, waits for them, and re-layouts: 47.9 us -> 15.9 us
  blocking collectives: 14.3 us -> 0 us
  between operations: 14.3 us -> 0.82 us
  matrix products: 12.2 us -> 25.1 us
  starting transfers between devices: 6.77 us -> 0 us
    psum x1 -> x0, waiting for transfers between devices: 142 us -> none  [local(): total = lax.psum(partial_grad, ('gx', 'gy'))]
    pallas_call x0 -> x2, Pallas kernels: none -> 72.9 us  [the longest x1 46 us: reduce_update(): pl.pallas_call(functools.partial(reduce_kernel, cube), out_shape=[jax.Sha...]
    all_to_all x2 -> x0, waiting for transfers between devices: 65.4 us -> none  [the longest x1 39.1 us: local(): lax.all_to_all(outgoing, ('gx', 'gy'), split_axis=0, concat_axis=0, tiled...]
    gather x6 -> x1, local copies, waits for them, and re-layouts: 24.8 us -> 8 us  [local(): rem_rows = lax.optimization_barrier(remainder_table[rem].astype(bf16))]
    sub x4 -> x1, other arithmetic: 17.5 us -> 2.69 us  [local(): new_remainder = remainder_table - update.reshape(r_rows, width).astype(f32)]
    all_to_all x1 -> x0, blocking collectives: 14.3 us -> none  [local(): lax.all_to_all(local_sent, ('gx', 'gy'), split_axis=0, concat_axis=0, til...]
    dot_general x5, matrix products: 12.2 us -> 25.1 us  [the longest x1 16.7 us: local(): jnp.dot(match(rem, jnp.arange(r_rows, dtype=jnp.int32)), r_terms, preferr...]
    scatter x2 -> x0, local copies, waits for them, and re-layouts: 10.5 us -> none  [the longest x1 5.26 us: local(): jnp.zeros((table_slots,), jnp.int32).at[target].set(local_row)]
  transfers between devices with their start and end apart: 4 -> 0, of which waited for: 4 -> 0; matrix products, arithmetic and copies ran while one was open for 7% -> 0% of each run, Pallas kernels for 0% -> 0%
where the time goes in v1:
time: 125 us; the launch traced here: 124 us
  Pallas kernels  72.9 us (58%)
  matrix products  25.1 us (20%)
  local copies, waits for them, and re-layouts  15.9 us (13%)
  other arithmetic  9.33 us (7%)
    pallas_call x1, Pallas kernels, reduce_update(): pl.pallas_call(functools.partial(reduce_kernel, cube), out_shape=[jax.Sha...  46 us
    pallas_call x1, Pallas kernels, gather_all(): pl.pallas_call(functools.partial(gather_kernel, cube), out_shape=outs, in...  26.8 us
    dot_general x1, matrix products, local(): jnp.dot(match(rem, jnp.arange(r_rows, dtype=jnp.int32)), r_terms, preferr...  16.7 us
    gather x1, local copies, waits for them, and re-layouts, local(): rem_rows = lax.optimization_barrier(remainder_table[rem].astype(bf16))  8 us
    dot_general x1, matrix products, local(): jnp.dot(match(row, wanted), q_terms, preferred_element_type=f32)  5.14 us
    another operation x5, other arithmetic  4.07 us
    unnamed x15, local copies, waits for them, and re-layouts  3.36 us
    sub x1, other arithmetic, local(): new_remainder = remainder_table - update.reshape(r_rows, width).astype(f32)  2.69 us

profile of v1, /device:TPU:0, one launch (start us, length us, event | category | flops | bytes accessed | tf_op | source)
XLA Modules:
  0.0 124.0 jit_solution(6850315345767668275)
XLA Ops:
  0.7 0.8 copy.13
  1.5 0.7 reshape.231.q
  2.2 0.8 copy.14
  3.0 0.7 reshape.232.r
  3.9 26.8 %gather_all.1 = (bf16[32,64,256]{2,1,0:T(8,128)(2,1)}, s32[32,1,1280]{2,1,0:T(1,128)}, s32[32,1,1280]{2,1,0:T(1,128)}) custom-call(bf16[64,256]{1,0:T(8,128)(2,1)} %cot.1, s32[1,1280]{1,0:T(1,128)} %reshape.231.q, s32[1,1280]{1,0:T(1,128)} %reshape.232.r), custom_call_target="tpu_custom_call" | custom-call | tf_op jit(solution)/shard_map/gather_all/pallas_call | solution.py:140
  30.8 1.3 %compare_and_fusion = pred[32,1,1280]{2,1,0:T(4,128)(4,1)S(1)} fusion(s32[32,1,1280]{2,1,0:T(1,128)} %get-tuple-element.9, s32[]{:T(128)S(6)} %mul.62), kind=kLoop, calls=%fused_computation.33 | loop fusion | flops 163840 | bytes 204804 | tf_op jit(solution)/shard_map/and | solution.py:303
  32.1 0.5 fusion.14
  32.6 2.3 %fusion.25 = (bf16[32,1,1280]{2,1,0:T(2,128)(2,1)S(1)}, s32[32,1,1280]{2,1,0:T(1,128)S(1)}, bf16[32,1,1280]{2,1,0:T(2,128)(2,1)S(1)}, s32[32,1,1280]{2,1,0:T(1,128)S(1)}) fusion(s32[32,1,1280]{2,1,0:T(1,128)} %get-tuple-element.9, s32[]{:T(128)S(6)} %mul.62, s32[32,1,1280]{2,1,0:T(1,128)} %get-tuple-element.10), kind=kLoop, calls=%fused_computation.47 | loop fusion | flops 1187840 | bytes 819204 | tf_op jit(solution)/shard_map/convert.2
  34.9 0.7 fusion.30
  35.6 0.9 fusion.29
  36.5 1.8 %stack.3 = bf16[32,6,1280]{2,1,0:T(8,128)(2,1)S(1)} concatenate(bf16[32,1,1280]{2,1,0:T(2,128)(2,1)S(1)} %fusion.29, bf16[32,1,1280]{2,1,0:T(2,128)(2,1)S(1)} %get-tuple-element.20, bf16[32,1,1280]{2,1,0:T(2,128)(2,1)S(1)} %fusion.30, bf16[32,1,1280]{2,1,0:T(2,128)(2,1)S(1)} %get-tuple-element.24, bf16[32,1,1280]{2,1,0:T(2,128)(2,1)S(1)} %fusion.23, bf16[32,1,1280]{2,1,0:T(2,128)(2,1)S(1)} %fusion.24), dimensions={1} | concatenate | bytes 983040 | tf_op jit(solution)/shard_map/stack | solution.py:312
  38.3 2.1 %fusion.16 = s32[6,32,80]{2,0,1:T(8,128)S(1)} fusion(bf16[32,6,1280]{2,1,0:T(8,128)(2,1)S(1)} %stack.3, s32[32,1280]{1,0:T(8,128)S(1)} %fusion.14), kind=kOutput, calls=%fused_computation.24 | convolution fusion | flops 42613760 | bytes 716800 | tf_op jit(solution)/shard_map/nvk,nck->vnc/dot_general | solution.py:315
  40.4 0.5 broadcast.276
  40.9 0.8 fusion.38
  41.8 0.7 add.128
  42.6 8.0 %gather_fusion = bf16[2560,256]{1,0:T(8,128)(2,1)S(1)} fusion(f32[4096,256]{1,0:T(8,128)} %param.9, s32[3072]{0:T(1024)S(1)} %pad_clamp_fusion), kind=kCustom, calls=%fused_computation | custom fusion | bytes 2631680 | tf_op jit(solution)/shard_map/gather | solution.py:322
  50.6 0.6 fusion.17
  51.2 0.4 fusion.12
  51.6 1.1 copy-done.2
  52.7 16.7 %fusion.9 = bf16[4096,256]{1,0:T(8,128)(2,1)S(1)} fusion(s32[2560]{0:T(1024)} %add.128, f32[2560,256]{1,0:T(8,128)} %bitcast.20, s32[2560]{0:T(1024)S(1)} %add.116, f32[1024,256]{1,0:T(8,128)} %param.7), kind=kOutput, calls=%fused_computation.15 | convolution fusion | flops 6726615040 | bytes 5787648 | tf_op jit(solution)/shard_map/dot_general | solution.py:331
  69.5 46.0 %reduce_update.1 = (f32[128,256]{1,0:T(8,128)S(1)}, bf16[32,128,256]{2,1,0:T(8,128)(2,1)S(1)}) custom-call(bf16[32,128,256]{2,1,0:T(8,128)(2,1)S(1)} %bitcast.19, f32[128,256]{1,0:T(8,128)S(1)} %copy-done), custom_call_target="tpu_custom_call" | custom-call | tf_op jit(solution)/shard_map/reduce_update/pallas_call | solution.py:248
  115.5 5.1 %divide_subtract_fusion = (f32[1024,256]{1,0:T(8,128)}, f32[1024,256]{1,0:T(8,128)}) fusion(f32[1024,256]{1,0:T(8,128)} %param.7, f32[1024,256]{1,0:T(8,128)} %param.8, bf16[2560,256]{1,0:T(8,128)(2,1)S(1)} %fusion.12, s32[2560]{0:T(1024)S(1)} %add.116), kind=kOutput, calls=%fused_computation.25 | convolution fusion | flops 1346371584 | bytes 5515264 | tf_op jit(solution)/shard_map/dot_general | solution.py:337
  120.7 2.7 %convert_subtract_fusion = f32[4096,256]{1,0:T(8,128)} fusion(f32[4096,256]{1,0:T(8,128)S(1)} %copy-done.1, bf16[32,128,256]{2,1,0:T(8,128)(2,1)S(1)} %get-tuple-element.12), kind=kLoop, calls=%fused_computation.16 | loop fusion | flops 2097152 | bytes 10485760 | tf_op jit(solution)/shard_map/sub | solution.py:339
  123.4 0.7 copy.21
  (22 shorter events, 0.5 us)
Async XLA Ops:
  30.8 4.1 %copy-start.5 = (s32[32,1,1280]{2,1,0:T(1,128)S(1)}, s32[32,1,1280]{2,1,0:T(1,128)}, u32[]{:S(2)}) copy-start(s32[32,1,1280]{2,1,0:T(1,128)} %get-tuple-element.10) | copy-start | bytes 491524
  30.8 4.8 %copy-start.3 = (s32[32,1,1280]{2,1,0:T(1,128)S(1)}, s32[32,1,1280]{2,1,0:T(1,128)}, u32[]{:S(2)}) copy-start(s32[32,1,1280]{2,1,0:T(1,128)} %get-tuple-element.9) | copy-start | bytes 491524
  42.6 8.0 %copy-start.4 = (bf16[32,64,256]{2,1,0:T(8,128)(2,1)S(1)}, bf16[32,64,256]{2,1,0:T(8,128)(2,1)}, u32[]{:S(2)}) copy-start(bf16[32,64,256]{2,1,0:T(8,128)(2,1)} %get-tuple-element.11) | copy-start | bytes 3145732
  51.2 1.5 %copy-start.2 = (f32[32,80,256]{2,1,0:T(8,128)}, f32[32,80,256]{2,1,0:T(8,128)S(1)}, u32[]{:S(2)}) copy-start(f32[32,80,256]{2,1,0:T(8,128)S(1)} %fusion.17) | copy-start | bytes 7864324
  52.7 16.7 %copy-start = (f32[128,256]{1,0:T(8,128)S(1)}, f32[128,256]{1,0:T(8,128)}, u32[]{:S(2)}) copy-start(f32[128,256]{1,0:T(8,128)} %acc.1) | copy-start | bytes 393220
  115.5 5.2 %copy-start.1 = (f32[4096,256]{1,0:T(8,128)S(1)}, f32[4096,256]{1,0:T(8,128)}, u32[]{:S(2)}) copy-start(f32[4096,256]{1,0:T(8,128)} %param.9) | copy-start | bytes 12582916

commit v2 on v1

--- a/solution.py
+++ b/solution.py
@@ -27,13 +27,25 @@
 
 
 class Cube:
-    def __init__(self, nx, ny, split):
+    def __init__(self, nx, ny, rows):
         gx = [("gx", w, w * ny) for w in weights(nx)]
-        gy = [("gy", w, w) for w in reversed(weights(ny))]
-        self.orders = [gx + gy]
-        if split:
-            self.orders.append(gx[:1] + gx[:0:-1] + gy)
+        gy = [("gy", w, w) for w in weights(ny)]
+        orders = [gx + gy, gx[:1] + gx[:0:-1] + gy, gx[:1] + gy + gx[1:]]
         self.bits = len(gx) + len(gy)
+        self.orders, self.spans = [], []
+        units = rows // 16
+        last = max(1, units // 4) if units >= 3 and rows % 16 == 0 else 0
+        if units < 2 or rows % 16:
+            sizes = [rows]
+        else:
+            sizes = [16 * ((units - last + 1) // 2), 16 * ((units - last) // 2), 16 * last]
+        start = 0
+        for order, size in zip(orders, sizes):
+            if size:
+                self.orders.append(order)
+                self.spans.append((start, size))
+                start += size
+        self.streams = len(self.orders)
 
     def locate(self):
         self.at = {"gx": lax.axis_index("gx"), "gy": lax.axis_index("gy")}
@@ -57,7 +69,19 @@
     def count(self, stage):
         return 2 ** (self.bits - 1 - stage)
 
-    def base(self, order, stage, flip):
+    def free(self, k, stage):
+        return sorted(self.orders[k][stage + 1 :], key=lambda e: -e[2])
+
+    def run(self, k, stage):
+        g = 1
+        for entry in reversed(self.free(k, stage)):
+            if entry[2] != g:
+                break
+            g *= 2
+        return g
+
+    def base(self, k, stage, flip):
+        order = self.orders[k]
         total = 0
         for t in range(stage + 1):
             b = self.bit(order[t])
@@ -66,31 +90,34 @@
             total = total + b * order[t][2]
         return total
 
-    def spread(self, order, stage, i):
-        free = order[stage + 1 :]
+    def spread(self, k, stage, i):
         total = 0
-        for t, entry in enumerate(free):
-            total += ((i >> (len(free) - 1 - t)) & 1) * entry[2]
+        for t, entry in enumerate(reversed(self.free(k, stage))):
+            total += ((i >> t) & 1) * entry[2]
         return total
 
-
-def spread_out(cube, streams, send_sems, recv_sems):
+    def child(self, k, stage, i):
+        free = self.free(k, stage - 1)
+        p = len(free) - 1 - free.index(self.orders[k][stage])
+        return ((i >> p) << (p + 1)) | (i & (2**p - 1)), 2**p
+
+
+def spread_out(cube, streams, send_sems, recv_sems, between=lambda stage: None):
     def copies(k, stage, flip):
-        order = cube.orders[k]
-        base = cube.base(order, stage, flip)
-        n = cube.count(stage)
+        base = cube.base(k, stage, flip)
+        n, g = cube.count(stage), cube.run(k, stage)
         out = []
-        for i in range(n):
-            block = base + cube.spread(order, stage, i)
+        for i in range(0, n, g):
+            block = base + cube.spread(k, stage, i)
             for m, view in enumerate(streams[k]):
-                ref = view(block)
+                ref = view(pl.ds(block, g))
                 out.append(
                     pltpu.make_async_remote_copy(
                         src_ref=ref,
                         dst_ref=ref,
                         send_sem=send_sems.at[k, m, n - 1 + i],
                         recv_sem=recv_sems.at[k, m, n - 1 + i],
-                        device_id=cube.partner(order[stage]),
+                        device_id=cube.partner(cube.orders[k][stage]),
                         device_id_type=MESH,
                     )
                 )
@@ -103,6 +130,7 @@
                     c.wait_recv()
             for c in copies(k, stage, False):
                 c.start()
+        between(stage)
     for k in range(len(streams)):
         for c in copies(k, 0, True):
             c.wait_recv()
@@ -124,17 +152,17 @@
     cube.greet()
     for c in own:
         c.wait()
-    half = cot.shape[0] // 2
     streams = [
-        [lambda b: cots.at[b, pl.ds(0, half)], lambda b: qs.at[b]],
-        [lambda b: cots.at[b, pl.ds(half, half)], lambda b: rs.at[b]],
+        [lambda b, lo=lo, size=size: cots.at[b, pl.ds(lo, size)]] for lo, size in cube.spans
     ]
+    streams[-1].append(lambda b: qs.at[b])
+    streams[-2 % cube.streams].append(lambda b: rs.at[b])
     spread_out(cube, streams, send_sems, recv_sems)
 
 
 def gather_all(nx, ny, cot, q, r):
     devices = nx * ny
-    cube = Cube(nx, ny, True)
+    cube = Cube(nx, ny, cot.shape[0])
     vm = pl.BlockSpec(memory_space=VMEM)
     outs = [jax.ShapeDtypeStruct((devices,) + x.shape, x.dtype) for x in (cot, q, r)]
     return pl.pallas_call(
@@ -143,8 +171,8 @@
         in_specs=[vm] * 3,
         out_specs=[vm] * 3,
         scratch_shapes=[
-            pltpu.SemaphoreType.DMA((2, 2, devices - 1)),
-            pltpu.SemaphoreType.DMA((2, 2, devices - 1)),
+            pltpu.SemaphoreType.DMA((cube.streams, 3, devices - 1)),
+            pltpu.SemaphoreType.DMA((cube.streams, 3, devices - 1)),
             pltpu.SemaphoreType.DMA((3,)),
         ],
         compiler_params=pltpu.CompilerParams(collective_id=0, has_side_effects=True),
@@ -158,92 +186,77 @@
     cube.locate()
     ny = lax.axis_size("gy")
     me = cube.at["gx"] * ny + cube.at["gy"]
-    streams = len(cube.orders)
-    rows = part.shape[1] // streams
     cube.greet()
 
-    def copy(k, stage, i, src):
-        slot = cube.count(stage) - 1 + i
+    def rows(k):
+        return pl.ds(*cube.spans[k])
+
+    def copy(k, stage, i):
+        n, g = cube.count(stage), cube.run(k, stage)
+        if stage == 0:
+            src = part.at[pl.ds(cube.base(k, 0, True) + cube.spread(k, 0, i), g), rows(k)]
+        else:
+            src = sent.at[pl.ds(n - 1 + i, g), rows(k)]
         return pltpu.make_async_remote_copy(
             src_ref=src,
-            dst_ref=landed.at[slot, pl.ds(k * rows, rows)],
-            send_sem=send_sems.at[k, slot],
-            recv_sem=recv_sems.at[k, slot],
+            dst_ref=landed.at[pl.ds(n - 1 + i, g), rows(k)],
+            send_sem=send_sems.at[k, n - 1 + i],
+            recv_sem=recv_sems.at[k, n - 1 + i],
             device_id=cube.partner(cube.orders[k][stage]),
             device_id_type=MESH,
         )
 
-    def source(k, stage, i):
-        if stage == 0:
-            order = cube.orders[k]
-            block = cube.base(order, 0, True) + cube.spread(order, 0, i)
-            return part.at[block, pl.ds(k * rows, rows)]
-        return sent.at[cube.count(stage) - 1 + i, pl.ds(k * rows, rows)]
-
-    def total(k, stage, i):
-        n = cube.count(stage)
-        order = cube.orders[k]
-        got = landed[n - 1 + i, pl.ds(k * rows, rows), :].astype(jnp.float32)
-        if stage == 0:
-            block = cube.base(order, 0, False) + i
-            mine = part[block, pl.ds(k * rows, rows), :].astype(jnp.float32)
-        else:
-            mine = held[n - 1 + i, pl.ds(k * rows, rows), :]
-        return mine + got
-
-    def stage0_total(k, b, low):
-        order = cube.orders[k]
-        n = cube.count(0)
-        half = n // 2
-        got = landed[n - 1 + b * half + low, pl.ds(k * rows, rows), :]
-        block = cube.base(order, 0, False) + b * order[1][2] + cube.spread(order, 1, low)
-        mine = part[block, pl.ds(k * rows, rows), :]
-        return mine.astype(jnp.float32) + got.astype(jnp.float32)
-
-    for k in range(streams):
-        for i in range(cube.count(0)):
-            copy(k, 0, i, source(k, 0, i)).start()
+    def copies(k, stage):
+        return [copy(k, stage, i) for i in range(0, cube.count(stage), cube.run(k, stage))]
+
+    def value(k, stage, side, i):
+        n = cube.count(stage - 1)
+        start, step = cube.child(k, stage, i)
+        at = n - 1 + start + side * step
+        got = landed[at, rows(k), :].astype(jnp.float32)
+        if stage == 1:
+            block = cube.base(k, 0, False) + cube.spread(k, 0, start)
+            block = block + side * cube.orders[k][1][2]
+            return part[block, rows(k), :].astype(jnp.float32) + got
+        return held[at, rows(k), :] + got
+
+    for k in range(cube.streams):
+        for c in copies(k, 0):
+            c.start()
     for stage in range(1, cube.bits):
         n = cube.count(stage)
-        for k in range(streams):
-            for i in range(2 * n):
-                copy(k, stage - 1, i, source(k, stage - 1, i)).wait_recv()
+        for k in range(cube.streams):
+            for c in copies(k, stage - 1):
+                c.wait_recv()
             b = cube.bit(cube.orders[k][stage])
-
-            def value(side, i, k=k, stage=stage, n=n):
-                if stage == 1:
-                    return stage0_total(k, side, i)
-                return total(k, stage - 1, side * n + i)
-
+            g = cube.run(k, stage)
             for i in range(n):
-                sent[n - 1 + i, pl.ds(k * rows, rows), :] = value(1 - b, i).astype(sent.dtype)
-                copy(k, stage, i, source(k, stage, i)).start()
+                sent[n - 1 + i, rows(k), :] = value(k, stage, 1 - b, i).astype(sent.dtype)
+                if (i + 1) % g == 0:
+                    copy(k, stage, i + 1 - g).start()
             for i in range(n):
-                held[n - 1 + i, pl.ds(k * rows, rows), :] = value(b, i)
+                held[n - 1 + i, rows(k), :] = value(k, stage, b, i)
     last = cube.bits - 1
-    for k in range(streams):
-        copy(k, last, 0, source(k, last, 0)).wait_recv()
-        grad = total(k, last, 0)
-        mine = pl.ds(k * rows, rows)
-        new = acc[mine, :] + grad * grad
-        fresh[mine, :] = new
+    for k in range(cube.streams):
+        copy(k, last, 0).wait_recv()
+        grad = held[0, rows(k), :] + landed[0, rows(k), :].astype(jnp.float32)
+        new = acc[rows(k), :] + grad * grad
+        fresh[rows(k), :] = new
         step = LEARNING_RATE * grad / (jnp.sqrt(new) + EPSILON)
-        update[me, mine, :] = step.astype(update.dtype)
-    views = [
-        [lambda b, k=k: update.at[b, pl.ds(k * rows, rows)]] for k in range(streams)
-    ]
+        update[me, rows(k), :] = step.astype(update.dtype)
+    views = [[lambda b, k=k: update.at[b, rows(k)]] for k in range(cube.streams)]
     spread_out(cube, views, ag_send, ag_recv)
-    for k in range(streams):
+    for k in range(cube.streams):
         for stage in range(cube.bits):
-            for i in range(cube.count(stage)):
-                copy(k, stage, i, source(k, stage, i)).wait_send()
+            for c in copies(k, stage):
+                c.wait_send()
 
 
 def reduce_update(nx, ny, part, acc):
     devices = nx * ny
     share, width = acc.shape
-    cube = Cube(nx, ny, share % 32 == 0)
-    k = len(cube.orders)
+    cube = Cube(nx, ny, share)
+    k = cube.streams
     vm = pl.BlockSpec(memory_space=VMEM)
     return pl.pallas_call(
         functools.partial(reduce_kernel, cube),
@@ -295,7 +308,7 @@
     f32, bf16 = jnp.float32, jnp.bfloat16
     me = lax.axis_index(("gx", "gy"))
     cots, qs, rs = gather_all(
-        nx, ny, cotangent, quotient_ids.reshape(1, count), remainder_ids.reshape(1, count)
+        nx, ny, cotangent, quotient_ids.T.reshape(1, count), remainder_ids.T.reshape(1, count)
     )
     qs = qs.reshape(devices, count)
     rs = rs.reshape(devices, count)
@@ -308,7 +321,7 @@
     seat = jnp.arange(capacity, dtype=jnp.int32)
     pick = (place[:, None, :] == seat[None, :, None]).astype(bf16)
     near = jnp.where(mine, near, 0)
-    sample = jnp.broadcast_to(steps // bag + 1, (devices, count))
+    sample = jnp.broadcast_to(steps % samples + 1, (devices, count))
     facts = jnp.stack(
         [near // 256, near % 256, rs // 256, rs % 256, sample // 128, sample % 128], axis=1
     ).astype(bf16)
@@ -328,9 +341,15 @@
     )
     q_terms = (cot_rows * rem_rows.astype(f32)).astype(bf16)
     r_terms = (cot_rows * q_rows).astype(bf16)
-    part = jnp.dot(
-        match(rem, jnp.arange(r_rows, dtype=jnp.int32)), r_terms, preferred_element_type=f32
-    ).astype(bf16)
+    r_terms = lax.optimization_barrier(r_terms)
+    tile = 256 if r_rows % 256 == 0 else r_rows
+    tiles = jnp.arange(r_rows // tile, dtype=jnp.int32)
+    inside = rem[None, :] - tile * tiles[:, None]
+    inside = jnp.where((inside >= 0) & (inside < tile), inside, -1).astype(bf16)
+    inside = lax.optimization_barrier(inside)
+    offset = jnp.arange(tile, dtype=jnp.int32).astype(bf16)
+    hit = (inside[:, None, :] == offset[None, :, None]).astype(bf16)
+    part = jnp.einsum("tis,sw->tiw", hit, r_terms, preferred_element_type=f32).astype(bf16)
     new_remainder_acc, update = reduce_update(
         nx, ny, part.reshape(devices, share, width), remainder_acc
     )

time: 125 us -> 112 us (0.90)
  matrix products: 25.1 us -> 16.2 us
  Pallas kernels: 72.9 us -> 70.3 us
    dot_general x1 -> x2, matrix products: 16.7 us -> 9.52 us  [the longest x1 7.1 us: local(): jnp.einsum('tis,sw->tiw', hit, r_terms, preferred_element_type=f32)]
    pallas_call x1, Pallas kernels: 46 us -> 42.5 us  [reduce_update(): pl.pallas_call(functools.partial(reduce_kernel, cube), out_shape=[jax.Sha...]
    unnamed x15, local copies, waits for them, and re-layouts: 3.36 us -> 1.52 us
    dot_general x1, matrix products: 5.14 us -> 3.45 us  [local(): jnp.dot(match(row, wanted), q_terms, preferred_element_type=f32)]
    reshape x2, local copies, waits for them, and re-layouts: 1.41 us -> 2.75 us  [the longest x1 1.38 us: local(): quotient_ids.T.reshape(1, count)]
where the time goes in v2:
time: 112 us
  Pallas kernels  70.3 us (63%)
  matrix products  16.2 us (14%)
  local copies, waits for them, and re-layouts  14.8 us (13%)
  other arithmetic  9.39 us (8%)
    pallas_call x1, Pallas kernels, reduce_update(): pl.pallas_call(functools.partial(reduce_kernel, cube), out_shape=[jax.Sha...  42.5 us
    pallas_call x1, Pallas kernels, gather_all(): pl.pallas_call(functools.partial(gather_kernel, cube), out_shape=outs, in...  27.7 us
    gather x1, local copies, waits for them, and re-layouts, local(): rem_rows = lax.optimization_barrier(remainder_table[rem].astype(bf16))  8 us
    dot_general x1, matrix products, local(): jnp.einsum('tis,sw->tiw', hit, r_terms, preferred_element_type=f32)  7.1 us
    another operation x5, other arithmetic  4.07 us
    dot_general x1, matrix products, local(): jnp.dot(match(row, wanted), q_terms, preferred_element_type=f32)  3.45 us
    sub x1, other arithmetic, local(): new_remainder = remainder_table - update.reshape(r_rows, width).astype(f32)  2.69 us
    dot_general x1, matrix products, local(): jnp.dot((row[:, None] == wanted[None, :]).astype(bf16), quotient_table.as...  2.42 us

profile of v2, /device:TPU:0, one launch (start us, length us, event | category | flops | bytes accessed | tf_op | source)
XLA Modules:
  0.0 111.5 jit_solution(5658749406161029464)
XLA Ops:
  0.7 1.4 %reshape.241.q = s32[1,1280]{1,0:T(1,128)} reshape(s32[20,64]{1,0:T(8,128)} %bitcast.28) | data formatting | bytes 10240 | tf_op jit(solution)/shard_map/reshape | solution.py:311
  2.1 1.4 %reshape.242.r = s32[1,1280]{1,0:T(1,128)} reshape(s32[20,64]{1,0:T(8,128)} %bitcast.29) | data formatting | bytes 10240 | tf_op jit(solution)/shard_map/reshape | solution.py:311
  3.5 0.1 fusion.28
  3.7 27.7 %gather_all.1 = (bf16[32,64,256]{2,1,0:T(8,128)(2,1)}, s32[32,1,1280]{2,1,0:T(1,128)}, s32[32,1,1280]{2,1,0:T(1,128)}) custom-call(bf16[64,256]{1,0:T(8,128)(2,1)} %cot.1, s32[1,1280]{1,0:T(1,128)} %reshape.241.q, s32[1,1280]{1,0:T(1,128)} %reshape.242.r), custom_call_target="tpu_custom_call" | custom-call | tf_op jit(solution)/shard_map/gather_all/pallas_call | solution.py:168
  31.4 1.3 %compare_and_fusion = pred[32,1,1280]{2,1,0:T(4,128)(4,1)S(1)} fusion(s32[32,1,1280]{2,1,0:T(1,128)} %get-tuple-element.9, s32[]{:T(128)S(6)} %mul.70), kind=kLoop, calls=%fused_computation.35 | loop fusion | flops 163840 | bytes 204804 | tf_op jit(solution)/shard_map/and | solution.py:316
  32.7 0.5 fusion.15
  33.2 2.3 %fusion.30 = (bf16[32,1,1280]{2,1,0:T(2,128)(2,1)S(1)}, s32[32,1,1280]{2,1,0:T(1,128)S(1)}, bf16[32,1,1280]{2,1,0:T(2,128)(2,1)S(1)}, s32[32,1,1280]{2,1,0:T(1,128)S(1)}) fusion(s32[32,1,1280]{2,1,0:T(1,128)} %get-tuple-element.9, s32[]{:T(128)S(6)} %mul.70, s32[32,1,1280]{2,1,0:T(1,128)} %get-tuple-element.10), kind=kLoop, calls=%fused_computation.53 | loop fusion | flops 1187840 | bytes 819204 | tf_op jit(solution)/shard_map/convert.2
  35.5 0.7 fusion.36
  36.2 0.9 fusion.35
  37.1 1.8 %stack.3 = bf16[32,6,1280]{2,1,0:T(8,128)(2,1)S(1)} concatenate(bf16[32,1,1280]{2,1,0:T(2,128)(2,1)S(1)} %fusion.35, bf16[32,1,1280]{2,1,0:T(2,128)(2,1)S(1)} %get-tuple-element.20, bf16[32,1,1280]{2,1,0:T(2,128)(2,1)S(1)} %fusion.36, bf16[32,1,1280]{2,1,0:T(2,128)(2,1)S(1)} %get-tuple-element.24, bf16[32,1,1280]{2,1,0:T(2,128)(2,1)S(1)} %fusion.28, bf16[32,1,1280]{2,1,0:T(2,128)(2,1)S(1)} %fusion.29), dimensions={1} | concatenate | bytes 983040 | tf_op jit(solution)/shard_map/stack | solution.py:325
  38.9 2.1 %fusion.21 = s32[6,32,80]{2,0,1:T(8,128)S(1)} fusion(bf16[32,6,1280]{2,1,0:T(8,128)(2,1)S(1)} %stack.3, s32[32,1280]{1,0:T(8,128)S(1)} %fusion.15), kind=kOutput, calls=%fused_computation.26 | convolution fusion | flops 42613760 | bytes 716800 | tf_op jit(solution)/shard_map/nvk,nck->vnc/dot_general | solution.py:328
  41.0 0.5 broadcast.276
  41.5 0.8 fusion.45
  42.6 0.1 fusion.27
  42.7 8.0 %gather_fusion = bf16[2560,256]{1,0:T(8,128)(2,1)S(1)} fusion(f32[4096,256]{1,0:T(8,128)} %param.9, s32[3072]{0:T(1024)S(1)} %pad_clamp_fusion), kind=kCustom, calls=%fused_computation | custom fusion | bytes 2631680 | tf_op jit(solution)/shard_map/gather | solution.py:335
  50.7 0.6 fusion.22
  51.4 0.4 fusion.13
  51.8 0.8 copy-done.5
  52.6 2.4 %fusion.12 = bf16[2560,256]{1,0:T(8,128)(2,1)S(1)} fusion(f32[2560,256]{1,0:T(8,128)S(1)} %bitcast.25, s32[2560]{0:T(1024)S(1)} %add.127, f32[1024,256]{1,0:T(8,128)S(1)} %copy-done.5), kind=kOutput, calls=%fused_computation.18 | convolution fusion | flops 1346371584 | bytes 4990976 | tf_op jit(solution)/shard_map/dot_general | solution.py:337
  55.0 7.1 %fusion.16 = bf16[16,256,256]{2,1,0:T(8,128)(2,1)S(1)} fusion(bf16[16,2560]{1,0:T(8,128)(2,1)S(1)} %fusion.27, bf16[256]{0:T(256)(128)(2,1)S(1)} %iota_convert_fusion, bf16[2560,256]{1,0:T(8,128)(2,1)S(1)} %fusion.12), kind=kOutput, calls=%fused_computation.23 | convolution fusion | flops 5380243456 | bytes 3490304 | tf_op jit(solution)/shard_map/tis,sw->tiw/dot_general | solution.py:352
  62.2 42.5 %reduce_update.1 = (f32[128,256]{1,0:T(8,128)S(1)}, bf16[32,128,256]{2,1,0:T(8,128)(2,1)S(1)}) custom-call(bf16[32,128,256]{2,1,0:T(8,128)(2,1)S(1)} %bitcast.24, f32[128,256]{1,0:T(8,128)S(1)} %copy-done), custom_call_target="tpu_custom_call" | custom-call | tf_op jit(solution)/shard_map/reduce_update/pallas_call | solution.py:261
  104.7 3.4 %divide_subtract_fusion = (f32[1024,256]{1,0:T(8,128)}, f32[1024,256]{1,0:T(8,128)}) fusion(f32[1024,256]{1,0:T(8,128)S(1)} %copy-done.5, f32[1024,256]{1,0:T(8,128)S(1)} %copy-done.6, bf16[2560,256]{1,0:T(8,128)(2,1)S(1)} %fusion.13, s32[2560]{0:T(1024)S(1)} %add.127), kind=kOutput, calls=%fused_computation.27 | convolution fusion | flops 1346371584 | bytes 5515264 | tf_op jit(solution)/shard_map/dot_general | solution.py:356
  108.2 2.7 %convert_subtract_fusion = f32[4096,256]{1,0:T(8,128)} fusion(f32[4096,256]{1,0:T(8,128)S(1)} %copy-done.1, bf16[32,128,256]{2,1,0:T(8,128)(2,1)S(1)} %get-tuple-element.12), kind=kLoop, calls=%fused_computation.16 | loop fusion | flops 2097152 | bytes 10485760 | tf_op jit(solution)/shard_map/sub | solution.py:358
  110.9 0.7 copy.17
  (26 shorter events, 0.4 us)
Async XLA Ops:
  31.4 4.1 %copy-start.4 = (s32[32,1,1280]{2,1,0:T(1,128)S(1)}, s32[32,1,1280]{2,1,0:T(1,128)}, u32[]{:S(2)}) copy-start(s32[32,1,1280]{2,1,0:T(1,128)} %get-tuple-element.10) | copy-start | bytes 491524
  31.4 4.8 %copy-start.2 = (s32[32,1,1280]{2,1,0:T(1,128)S(1)}, s32[32,1,1280]{2,1,0:T(1,128)}, u32[]{:S(2)}) copy-start(s32[32,1,1280]{2,1,0:T(1,128)} %get-tuple-element.9) | copy-start | bytes 491524
  42.7 8.0 %copy-start.3 = (bf16[32,64,256]{2,1,0:T(8,128)(2,1)S(1)}, bf16[32,64,256]{2,1,0:T(8,128)(2,1)}, u32[]{:S(2)}) copy-start(bf16[32,64,256]{2,1,0:T(8,128)(2,1)} %get-tuple-element.11) | copy-start | bytes 3145732
  51.4 1.2 %copy-start.5 = (f32[1024,256]{1,0:T(8,128)S(1)}, f32[1024,256]{1,0:T(8,128)}, u32[]{:S(2)}) copy-start(f32[1024,256]{1,0:T(8,128)} %param.7) | copy-start | bytes 3145732
  55.0 7.1 %copy-start = (f32[128,256]{1,0:T(8,128)S(1)}, f32[128,256]{1,0:T(8,128)}, u32[]{:S(2)}) copy-start(f32[128,256]{1,0:T(8,128)} %acc.1) | copy-start | bytes 393220
  55.0 49.7 %copy-start.6 = (f32[1024,256]{1,0:T(8,128)S(1)}, f32[1024,256]{1,0:T(8,128)}, u32[]{:S(2)}) copy-start(f32[1024,256]{1,0:T(8,128)} %param.8) | copy-start | bytes 3145732
  104.7 3.5 %copy-start.1 = (f32[4096,256]{1,0:T(8,128)S(1)}, f32[4096,256]{1,0:T(8,128)}, u32[]{:S(2)}) copy-start(f32[4096,256]{1,0:T(8,128)} %param.9) | copy-start | bytes 12582916

commit v3 on v2

--- a/solution.py
+++ b/solution.py
@@ -181,8 +181,30 @@
 
 
 def reduce_kernel(
-    cube, part, acc, fresh, update, held, sent, landed, send_sems, recv_sems, ag_send, ag_recv
+    cube,
+    part,
+    acc,
+    table,
+    rem,
+    row,
+    cot_rows,
+    fresh,
+    update,
+    grads,
+    held,
+    sent,
+    landed,
+    wide,
+    narrow,
+    send_sems,
+    recv_sems,
+    ag_send,
+    ag_recv,
+    table_sem,
 ):
+    fetch = pltpu.make_async_copy(table, wide, table_sem)
+    fetch.start()
+
     cube.locate()
     ny = lax.axis_size("gy")
     me = cube.at["gx"] * ny + cube.at["gy"]
@@ -220,9 +242,35 @@
             return part[block, rows(k), :].astype(jnp.float32) + got
         return held[at, rows(k), :] + got
 
+    slots = rem.shape[0]
+    piece = 256 if slots % 256 == 0 else slots
+    pieces = slots // piece
+    gaps = 2 * cube.bits
+
+    def quotient_piece(p):
+        at = pl.ds(p * piece, piece)
+        names = lax.broadcasted_iota(jnp.int32, (piece, table.shape[0]), 1)
+        pick = (names == rem[at, :]).astype(jnp.bfloat16)
+        found = jnp.dot(pick, narrow[...], preferred_element_type=jnp.float32)
+        terms = (cot_rows[at, :].astype(jnp.float32) * found).astype(jnp.bfloat16)
+        names = lax.broadcasted_iota(jnp.int32, (grads.shape[0], piece), 0)
+        spot = (names == row[:, at]).astype(jnp.bfloat16)
+        sums = jnp.dot(spot, terms, preferred_element_type=jnp.float32)
+        if p == 0:
+            grads[...] = sums
+        else:
+            grads[...] += sums
+
+    def gap(g):
+        for p in range(g * pieces // gaps, (g + 1) * pieces // gaps):
+            quotient_piece(p)
+
     for k in range(cube.streams):
         for c in copies(k, 0):
             c.start()
+    fetch.wait()
+    narrow[...] = wide[...].astype(jnp.bfloat16)
+    gap(0)
     for stage in range(1, cube.bits):
         n = cube.count(stage)
         for k in range(cube.streams):
@@ -236,6 +284,7 @@
                     copy(k, stage, i + 1 - g).start()
             for i in range(n):
                 held[n - 1 + i, rows(k), :] = value(k, stage, b, i)
+        gap(stage)
     last = cube.bits - 1
     for k in range(cube.streams):
         copy(k, last, 0).wait_recv()
@@ -245,14 +294,14 @@
         step = LEARNING_RATE * grad / (jnp.sqrt(new) + EPSILON)
         update[me, rows(k), :] = step.astype(update.dtype)
     views = [[lambda b, k=k: update.at[b, rows(k)]] for k in range(cube.streams)]
-    spread_out(cube, views, ag_send, ag_recv)
+    spread_out(cube, views, ag_send, ag_recv, lambda stage: gap(gaps - 1 - stage))
     for k in range(cube.streams):
         for stage in range(cube.bits):
             for c in copies(k, stage):
                 c.wait_send()
 
 
-def reduce_update(nx, ny, part, acc):
+def reduce_update(nx, ny, part, acc, table, rem, row, cot_rows, q_dev):
     devices = nx * ny
     share, width = acc.shape
     cube = Cube(nx, ny, share)
@@ -263,27 +312,27 @@
         out_shape=[
             jax.ShapeDtypeStruct(acc.shape, jnp.float32),
             jax.ShapeDtypeStruct(part.shape, jnp.bfloat16),
+            jax.ShapeDtypeStruct((q_dev, width), jnp.float32),
         ],
-        in_specs=[vm] * 2,
-        out_specs=[vm] * 2,
+        in_specs=[vm, vm, pl.BlockSpec(memory_space=pl.ANY), vm, vm, vm],
+        out_specs=[vm] * 3,
         scratch_shapes=[
             pltpu.VMEM((devices // 2, share, width), jnp.float32),
             pltpu.VMEM((devices // 2, share, width), jnp.bfloat16),
             pltpu.VMEM((devices - 1, share, width), jnp.bfloat16),
+            pltpu.VMEM(table.shape, jnp.float32),
+            pltpu.VMEM(table.shape, jnp.bfloat16),
             pltpu.SemaphoreType.DMA((k, devices - 1)),
             pltpu.SemaphoreType.DMA((k, devices - 1)),
             pltpu.SemaphoreType.DMA((k, 1, devices - 1)),
             pltpu.SemaphoreType.DMA((k, 1, devices - 1)),
+            pltpu.SemaphoreType.DMA,
         ],
         compiler_params=pltpu.CompilerParams(
             collective_id=1, has_side_effects=True, vmem_limit_bytes=48 * 2**20
         ),
         name="reduce_update",
-    )(part, acc)
-
-
-def match(ids, wanted):
-    return (wanted[:, None] == ids[None, :]).astype(jnp.bfloat16)
+    )(part, acc, table, rem, row, cot_rows)
 
 
 def local(
@@ -332,14 +381,12 @@
     whose = (who[:, :, None] == 1 + jnp.arange(samples, dtype=jnp.int32)).astype(bf16)
     cot_rows = jnp.einsum("ncs,nsw->ncw", whose, cots, preferred_element_type=f32)
     cot_rows = cot_rows.reshape(slots, width)
-    rem_rows = lax.optimization_barrier(remainder_table[rem].astype(bf16))
     wanted = jnp.arange(q_dev, dtype=jnp.int32)
     q_rows = jnp.dot(
         (row[:, None] == wanted[None, :]).astype(bf16),
         quotient_table.astype(bf16),
         preferred_element_type=f32,
     )
-    q_terms = (cot_rows * rem_rows.astype(f32)).astype(bf16)
     r_terms = (cot_rows * q_rows).astype(bf16)
     r_terms = lax.optimization_barrier(r_terms)
     tile = 256 if r_rows % 256 == 0 else r_rows
@@ -350,10 +397,17 @@
     offset = jnp.arange(tile, dtype=jnp.int32).astype(bf16)
     hit = (inside[:, None, :] == offset[None, :, None]).astype(bf16)
     part = jnp.einsum("tis,sw->tiw", hit, r_terms, preferred_element_type=f32).astype(bf16)
-    new_remainder_acc, update = reduce_update(
-        nx, ny, part.reshape(devices, share, width), remainder_acc
+    new_remainder_acc, update, quotient_grad = reduce_update(
+        nx,
+        ny,
+        part.reshape(devices, share, width),
+        remainder_acc,
+        remainder_table,
+        rem.reshape(slots, 1),
+        row.reshape(1, slots),
+        cot_rows.astype(bf16),
+        q_dev,
     )
-    quotient_grad = jnp.dot(match(row, wanted), q_terms, preferred_element_type=f32)
     new_quotient, new_quotient_acc = adagrad(quotient_table, quotient_acc, quotient_grad)
     new_remainder = remainder_table - update.reshape(r_rows, width).astype(f32)
     return (new_quotient, new_quotient_acc, new_remainder, new_remainder_acc)

time: 112 us -> 112 us (level)
  local copies, waits for them, and re-layouts: 14.8 us -> 6.66 us
  Pallas kernels: 70.3 us -> 73.4 us
  matrix products: 16.2 us -> 18.9 us
  other arithmetic: 9.39 us -> 11.6 us
    gather x1 -> x0, local copies, waits for them, and re-layouts: 8 us -> none  [local(): rem_rows = lax.optimization_barrier(remainder_table[rem].astype(bf16))]
    dot_general x1 -> x0, matrix products: 3.45 us -> none  [local(): jnp.dot(match(row, wanted), q_terms, preferred_element_type=f32)]
    pallas_call x1, Pallas kernels: 42.5 us -> 45.7 us  [reduce_update(): pl.pallas_call(functools.partial(reduce_kernel, cube), out_shape=[jax.Sha...]
    dot_general x1, matrix products: 2.42 us -> 5.24 us  [local(): jnp.dot((row[:, None] == wanted[None, :]).astype(bf16), quotient_table.as...]
    dot_general x1, matrix products: 7.1 us -> 9.3 us  [local(): jnp.einsum('tis,sw->tiw', hit, r_terms, preferred_element_type=f32)]
    another operation x5, other arithmetic: 4.07 us -> 5.93 us
    sub x0 -> x1, other arithmetic: none -> 1.78 us  [adagrad(): return (param - LEARNING_RATE * grad / (jnp.sqrt(fresh) + EPSILON), fresh)]
    dot_general x1, matrix products: 0.63 us -> 1.85 us  [local(): jnp.einsum('ncs,nsw->ncw', whose, cots, preferred_element_type=f32)]
where the time goes in v3:
time: 112 us
  Pallas kernels  73.4 us (66%)
  matrix products  18.9 us (17%)
  other arithmetic  11.6 us (10%)
  local copies, waits for them, and re-layouts  6.66 us (6%)
    pallas_call x1, Pallas kernels, reduce_update(): pl.pallas_call(functools.partial(reduce_kernel, cube), out_shape=[jax.Sha...  45.7 us
    pallas_call x1, Pallas kernels, gather_all(): pl.pallas_call(functools.partial(gather_kernel, cube), out_shape=outs, in...  27.7 us
    dot_general x1, matrix products, local(): jnp.einsum('tis,sw->tiw', hit, r_terms, preferred_element_type=f32)  9.3 us
    another operation x5, other arithmetic  5.93 us
    dot_general x1, matrix products, local(): jnp.dot((row[:, None] == wanted[None, :]).astype(bf16), quotient_table.as...  5.24 us
    sub x1, other arithmetic, local(): new_remainder = remainder_table - update.reshape(r_rows, width).astype(f32)  2.56 us

profile of v3, /device:TPU:0, one launch (start us, length us, event | category | flops | bytes accessed | tf_op | source)
XLA Modules:
  0.0 111.5 jit_solution(6226846408552308337)
XLA Ops:
  0.6 1.4 %reshape.242.q = s32[1,1280]{1,0:T(1,128)} reshape(s32[20,64]{1,0:T(8,128)} %bitcast.28) | data formatting | bytes 10240 | tf_op jit(solution)/shard_map/reshape | solution.py:360
  2.0 1.4 %reshape.243.r = s32[1,1280]{1,0:T(1,128)} reshape(s32[20,64]{1,0:T(8,128)} %bitcast.29) | data formatting | bytes 10240 | tf_op jit(solution)/shard_map/reshape | solution.py:360
  3.4 27.7 %gather_all.1 = (bf16[32,64,256]{2,1,0:T(8,128)(2,1)}, s32[32,1,1280]{2,1,0:T(1,128)}, s32[32,1,1280]{2,1,0:T(1,128)}) custom-call(bf16[64,256]{1,0:T(8,128)(2,1)} %cot.1, s32[1,1280]{1,0:T(1,128)} %reshape.242.q, s32[1,1280]{1,0:T(1,128)} %reshape.243.r), custom_call_target="tpu_custom_call" | custom-call | tf_op jit(solution)/shard_map/gather_all/pallas_call | solution.py:168
  31.1 2.3 %fusion.27 = (bf16[32,1,1280]{2,1,0:T(2,128)(2,1)S(1)}, s32[32,1,1280]{2,1,0:T(1,128)S(1)}, bf16[32,1,1280]{2,1,0:T(2,128)(2,1)S(1)}, s32[32,1,1280]{2,1,0:T(1,128)S(1)}) fusion(s32[32,1,1280]{2,1,0:T(1,128)} %get-tuple-element.10, s32[]{:T(128)S(6)} %mul.70, s32[32,1,1280]{2,1,0:T(1,128)} %get-tuple-element.11), kind=kLoop, calls=%fused_computation.48 | loop fusion | flops 1187840 | bytes 819204 | tf_op jit(solution)/shard_map/convert.2
  33.5 1.8 %fusion.32 = bf16[32,1,1280]{2,1,0:T(2,128)(2,1)S(1)} fusion(s32[32,1,1280]{2,1,0:T(1,128)S(1)} %get-tuple-element.25, s32[32,1,1280]{2,1,0:T(1,128)} %get-tuple-element.10, s32[]{:T(128)S(6)} %mul.70), kind=kLoop, calls=%fused_computation.53 | loop fusion | flops 737280 | bytes 409604 | tf_op jit(solution)/shard_map/convert.1
  35.3 1.6 %fusion.33 = bf16[32,1,1280]{2,1,0:T(2,128)(2,1)S(1)} fusion(s32[32,1,1280]{2,1,0:T(1,128)} %get-tuple-element.11, s32[32,1,1280]{2,1,0:T(1,128)S(1)} %get-tuple-element.30), kind=kLoop, calls=%fused_computation.54 | loop fusion | flops 532480 | bytes 409600 | tf_op jit(solution)/shard_map/convert.3
  36.9 0.1 fusion.25
  37.0 0.1 fusion.26
  37.1 1.8 %stack.3 = bf16[32,6,1280]{2,1,0:T(8,128)(2,1)S(1)} concatenate(bf16[32,1,1280]{2,1,0:T(2,128)(2,1)S(1)} %fusion.32, bf16[32,1,1280]{2,1,0:T(2,128)(2,1)S(1)} %get-tuple-element.24, bf16[32,1,1280]{2,1,0:T(2,128)(2,1)S(1)} %fusion.33, bf16[32,1,1280]{2,1,0:T(2,128)(2,1)S(1)} %get-tuple-element.29, bf16[32,1,1280]{2,1,0:T(2,128)(2,1)S(1)} %fusion.25, bf16[32,1,1280]{2,1,0:T(2,128)(2,1)S(1)} %fusion.26), dimensions={1} | concatenate | bytes 983040 | tf_op jit(solution)/shard_map/stack | solution.py:374
  38.9 0.3 compare_and_fusion
  39.2 0.5 fusion.12
  39.7 2.1 %fusion.18 = s32[6,32,80]{2,0,1:T(8,128)S(1)} fusion(bf16[32,6,1280]{2,1,0:T(8,128)(2,1)S(1)} %stack.3, s32[32,1280]{1,0:T(8,128)S(1)} %fusion.12), kind=kOutput, calls=%fused_computation.21 | convolution fusion | flops 42613760 | bytes 716800 | tf_op jit(solution)/shard_map/nvk,nck->vnc/dot_general | solution.py:377
  41.8 0.5 broadcast.263
  42.3 0.8 fusion.40
  43.1 1.9 %fusion.19 = f32[32,80,256]{2,1,0:T(8,128)S(1)} fusion(bf16[32,64,256]{2,1,0:T(8,128)(2,1)} %get-tuple-element.12, s32[32,80]{1,0:T(8,128)S(1)} %bitcast.25, s32[64]{0:T(128)S(1)} %iota_add_fusion), kind=kOutput, calls=%fused_computation.24 | convolution fusion | flops 84049920 | bytes 3680512 | tf_op jit(solution)/shard_map/ncs,nsw->ncw/dot_general | solution.py:382
  45.1 5.2 %fusion.10 = bf16[2560,256]{1,0:T(8,128)(2,1)} fusion(f32[2560,256]{1,0:T(8,128)S(1)} %bitcast.23, s32[2560]{0:T(1024)S(1)} %add.125, f32[1024,256]{1,0:T(8,128)} %param.7), kind=kOutput, calls=%fused_computation.14 | convolution fusion | flops 1346371584 | bytes 4990976 | tf_op jit(solution)/shard_map/dot_general | solution.py:385
  50.4 0.1 fusion.24
  50.5 9.3 %fusion.13 = bf16[16,256,256]{2,1,0:T(8,128)(2,1)} fusion(bf16[16,2560]{1,0:T(8,128)(2,1)S(1)} %fusion.24, bf16[256]{0:T(256)(128)(2,1)S(1)} %iota_convert_fusion, bf16[2560,256]{1,0:T(8,128)(2,1)} %fusion.10), kind=kOutput, calls=%fused_computation.18 | convolution fusion | flops 5380243456 | bytes 3490304 | tf_op jit(solution)/shard_map/tis,sw->tiw/dot_general | solution.py:399
  59.8 0.1 bitcast_convert_fusion.cot_rows
  60.0 0.6 add.131.rem
  60.7 45.7 %reduce_update.1 = (f32[128,256]{1,0:T(8,128)S(1)}, bf16[32,128,256]{2,1,0:T(8,128)(2,1)S(1)}, f32[1024,256]{1,0:T(8,128)S(1)}) custom-call(bf16[32,128,256]{2,1,0:T(8,128)(2,1)} %bitcast.24, f32[128,256]{1,0:T(8,128)S(1)} %copy-done, f32[4096,256]{1,0:T(8,128)} %table.1, s32[2560,1]{1,0:T(8,128)S(1)} %add.131.rem, s32[1,2560]{1,0:T(1,128)S(1)} %add.127.row, ...), custom_call_target="tpu_custom_call" | custom-call | tf_op jit(solution)/shard_map/reduce_update/pallas_call | solution.py:310
  106.5 2.6 %convert_subtract_fusion = f32[4096,256]{1,0:T(8,128)} fusion(f32[4096,256]{1,0:T(8,128)S(1)} %copy-done.1, bf16[32,128,256]{2,1,0:T(8,128)(2,1)S(1)} %get-tuple-element.14), kind=kLoop, calls=%fused_computation.12 | loop fusion | flops 2097152 | bytes 10485760 | tf_op jit(solution)/shard_map/sub | solution.py:412
  109.1 1.8 %divide_subtract_fusion = (f32[1024,256]{1,0:T(8,128)}, f32[1024,256]{1,0:T(8,128)}) fusion(f32[1024,256]{1,0:T(8,128)S(1)} %copy-done.5, f32[1024,256]{1,0:T(8,128)S(1)} %get-tuple-element.13, f32[1024,256]{1,0:T(8,128)S(1)} %copy-done.6), kind=kLoop, calls=%fused_computation.22 | loop fusion | flops 1572864 | bytes 5242880 | tf_op jit(solution)/shard_map/sub | solution.py:18
  110.9 0.7 copy.18
  (24 shorter events, 0.4 us)
Async XLA Ops:
  31.1 7.8 %copy-start.4 = (s32[32,1,1280]{2,1,0:T(1,128)S(1)}, s32[32,1,1280]{2,1,0:T(1,128)}, u32[]{:S(2)}) copy-start(s32[32,1,1280]{2,1,0:T(1,128)} %get-tuple-element.10) | copy-start | bytes 491524
  45.0 5.3 %copy-start.2 = (f32[32,80,256]{2,1,0:T(8,128)}, f32[32,80,256]{2,1,0:T(8,128)S(1)}, u32[]{:S(2)}) copy-start(f32[32,80,256]{2,1,0:T(8,128)S(1)} %fusion.19) | copy-start | bytes 7864324
  50.5 9.3 %copy-start.3 = (f32[32,80,256]{2,1,0:T(8,128)S(1)}, f32[32,80,256]{2,1,0:T(8,128)}, u32[]{:S(2)}) copy-start(f32[32,80,256]{2,1,0:T(8,128)} %copy-done.2) | copy-start | bytes 7864324
  59.8 0.9 copy-start
  60.7 45.8 %copy-start.1 = (f32[4096,256]{1,0:T(8,128)S(1)}, f32[4096,256]{1,0:T(8,128)}, u32[]{:S(2)}) copy-start(f32[4096,256]{1,0:T(8,128)} %table.1) | copy-start | bytes 12582916
  106.5 2.6 %copy-start.5 = (f32[1024,256]{1,0:T(8,128)S(1)}, f32[1024,256]{1,0:T(8,128)}, u32[]{:S(2)}) copy-start(f32[1024,256]{1,0:T(8,128)} %param.7) | copy-start | bytes 3145732
  106.5 2.6 %copy-start.6 = (f32[1024,256]{1,0:T(8,128)S(1)}, f32[1024,256]{1,0:T(8,128)}, u32[]{:S(2)}) copy-start(f32[1024,256]{1,0:T(8,128)} %param.8) | copy-start | bytes 3145732

commit v4 on v3

--- a/solution.py
+++ b/solution.py
@@ -175,7 +175,9 @@
             pltpu.SemaphoreType.DMA((cube.streams, 3, devices - 1)),
             pltpu.SemaphoreType.DMA((3,)),
         ],
-        compiler_params=pltpu.CompilerParams(collective_id=0, has_side_effects=True),
+        compiler_params=pltpu.CompilerParams(
+            collective_id=0, has_side_effects=True, vmem_limit_bytes=8 * 2**20
+        ),
         name="gather_all",
     )(cot, q, r)
 
@@ -329,7 +331,7 @@
             pltpu.SemaphoreType.DMA,
         ],
         compiler_params=pltpu.CompilerParams(
-            collective_id=1, has_side_effects=True, vmem_limit_bytes=48 * 2**20
+            collective_id=1, has_side_effects=True, vmem_limit_bytes=28 * 2**20
         ),
         name="reduce_update",
     )(part, acc, table, rem, row, cot_rows)

time: 112 us -> 107 us (0.955)
  Pallas kernels: 73.4 us -> 68.5 us
  local copies, waits for them, and re-layouts: 6.66 us -> 10 us
  other arithmetic: 11.6 us -> 8.91 us
    unnamed x15 -> x19, local copies, waits for them, and re-layouts: 0.77 us -> 5.3 us
    pallas_call x1, Pallas kernels: 45.7 us -> 42.7 us  [reduce_update(): pl.pallas_call(functools.partial(reduce_kernel, cube), out_shape=[jax.Sha...]
    another operation x5, other arithmetic: 5.93 us -> 3.07 us
    pallas_call x1, Pallas kernels: 27.7 us -> 25.8 us  [gather_all(): pl.pallas_call(functools.partial(gather_kernel, cube), out_shape=outs, in...]
where the time goes in v4:
time: 107 us
  Pallas kernels  68.5 us (64%)
  matrix products  18.7 us (17%)
  local copies, waits for them, and re-layouts  10 us (9%)
  other arithmetic  8.91 us (8%)
    pallas_call x1, Pallas kernels, reduce_update(): pl.pallas_call(functools.partial(reduce_kernel, cube), out_shape=[jax.Sha...  42.7 us
    pallas_call x1, Pallas kernels, gather_all(): pl.pallas_call(functools.partial(gather_kernel, cube), out_shape=outs, in...  25.8 us
    dot_general x1, matrix products, local(): jnp.einsum('tis,sw->tiw', hit, r_terms, preferred_element_type=f32)  9.46 us
    unnamed x19, local copies, waits for them, and re-layouts  5.3 us
    dot_general x1, matrix products, local(): jnp.dot((row[:, None] == wanted[None, :]).astype(bf16), quotient_table.as...  4.55 us
    another operation x5, other arithmetic  3.07 us
    sub x1, other arithmetic, local(): new_remainder = remainder_table - update.reshape(r_rows, width).astype(f32)  2.7 us

profile of v4, /device:TPU:0, one launch (start us, length us, event | category | flops | bytes accessed | tf_op | source)
XLA Modules:
  0.0 106.9 jit_solution(17818502047159003490)
XLA Ops:
  0.6 0.8 reshape.242.q
  1.4 0.8 reshape.243.r
  2.2 0.8 copy-done.4
  3.0 25.8 %gather_all.1 = (bf16[32,64,256]{2,1,0:T(8,128)(2,1)S(1)}, s32[32,1,1280]{2,1,0:T(1,128)S(1)}, s32[32,1,1280]{2,1,0:T(1,128)S(1)}) custom-call(bf16[64,256]{1,0:T(8,128)(2,1)S(1)} %copy-done.4, s32[1,1280]{1,0:T(1,128)S(1)} %reshape.242.q, s32[1,1280]{1,0:T(1,128)S(1)} %reshape.243.r), custom_call_target="tpu_custom_call" | custom-call | tf_op jit(solution)/shard_map/gather_all/pallas_call | solution.py:168
  28.8 1.3 %fusion.27 = (bf16[32,1,1280]{2,1,0:T(2,128)(2,1)S(1)}, s32[32,1,1280]{2,1,0:T(1,128)S(1)}, bf16[32,1,1280]{2,1,0:T(2,128)(2,1)S(1)}, s32[32,1,1280]{2,1,0:T(1,128)S(1)}) fusion(s32[32,1,1280]{2,1,0:T(1,128)S(1)} %get-tuple-element.10, s32[]{:T(128)S(6)} %mul.70, s32[32,1,1280]{2,1,0:T(1,128)S(1)} %get-tuple-element.11), kind=kLoop, calls=%fused_computation.48 | loop fusion | flops 1187840 | bytes 819204 | tf_op jit(solution)/shard_map/convert.2
  30.1 0.9 fusion.32
  31.0 0.7 fusion.33
  32.0 1.8 %stack.3 = bf16[32,6,1280]{2,1,0:T(8,128)(2,1)S(1)} concatenate(bf16[32,1,1280]{2,1,0:T(2,128)(2,1)S(1)} %fusion.32, bf16[32,1,1280]{2,1,0:T(2,128)(2,1)S(1)} %get-tuple-element.24, bf16[32,1,1280]{2,1,0:T(2,128)(2,1)S(1)} %fusion.33, bf16[32,1,1280]{2,1,0:T(2,128)(2,1)S(1)} %get-tuple-element.29, bf16[32,1,1280]{2,1,0:T(2,128)(2,1)S(1)} %fusion.25, bf16[32,1,1280]{2,1,0:T(2,128)(2,1)S(1)} %fusion.26), dimensions={1} | concatenate | bytes 983040 | tf_op jit(solution)/shard_map/stack | solution.py:376
  33.8 0.3 compare_and_fusion
  34.1 0.5 fusion.12
  34.6 2.1 %fusion.18 = s32[6,32,80]{2,0,1:T(8,128)S(1)} fusion(bf16[32,6,1280]{2,1,0:T(8,128)(2,1)S(1)} %stack.3, s32[32,1280]{1,0:T(8,128)S(1)} %fusion.12), kind=kOutput, calls=%fused_computation.21 | convolution fusion | flops 42613760 | bytes 716800 | tf_op jit(solution)/shard_map/nvk,nck->vnc/dot_general | solution.py:379
  36.6 0.5 broadcast.263
  37.1 0.8 fusion.40
  38.0 2.1 %fusion.19 = f32[32,80,256]{2,1,0:T(8,128)} fusion(bf16[32,64,256]{2,1,0:T(8,128)(2,1)S(1)} %get-tuple-element.12, s32[32,80]{1,0:T(8,128)S(1)} %bitcast.25, s32[64]{0:T(128)S(1)} %iota_add_fusion), kind=kOutput, calls=%fused_computation.24 | convolution fusion | flops 84049920 | bytes 3680512 | tf_op jit(solution)/shard_map/ncs,nsw->ncw/dot_general | solution.py:384
  40.2 4.5 %fusion.10 = bf16[2560,256]{1,0:T(8,128)(2,1)} fusion(f32[2560,256]{1,0:T(8,128)} %bitcast.24, s32[2560]{0:T(1024)S(1)} %add.125, f32[1024,256]{1,0:T(8,128)S(1)} %copy-done.6), kind=kOutput, calls=%fused_computation.14 | convolution fusion | flops 1346371584 | bytes 4990976 | tf_op jit(solution)/shard_map/dot_general | solution.py:387
  44.9 9.5 %fusion.13 = bf16[16,256,256]{2,1,0:T(8,128)(2,1)} fusion(bf16[16,2560]{1,0:T(8,128)(2,1)S(1)} %fusion.24, bf16[256]{0:T(256)(128)(2,1)S(1)} %iota_convert_fusion, bf16[2560,256]{1,0:T(8,128)(2,1)} %fusion.10), kind=kOutput, calls=%fused_computation.18 | convolution fusion | flops 5380243456 | bytes 3490304 | tf_op jit(solution)/shard_map/tis,sw->tiw/dot_general | solution.py:401
  54.4 0.1 bitcast_convert_fusion.cot_rows
  54.5 0.6 add.131.rem
  55.3 2.2 %copy-done = f32[4096,256]{1,0:T(8,128)S(1)} copy-done((f32[4096,256]{1,0:T(8,128)S(1)}, f32[4096,256]{1,0:T(8,128)}, u32[]{:S(2)}) %copy-start) | copy-done | bytes 4194328
  57.5 1.6 %copy-done.2 = bf16[16,256,256]{2,1,0:T(8,128)(2,1)S(1)} copy-done((bf16[16,256,256]{2,1,0:T(8,128)(2,1)S(1)}, bf16[16,256,256]{2,1,0:T(8,128)(2,1)}, u32[]{:S(2)}) %copy-start.2) | copy-done | bytes 2097176
  59.1 42.7 %reduce_update.1 = (f32[128,256]{1,0:T(8,128)S(1)}, bf16[32,128,256]{2,1,0:T(8,128)(2,1)S(1)}, f32[1024,256]{1,0:T(8,128)S(1)}) custom-call(bf16[32,128,256]{2,1,0:T(8,128)(2,1)S(1)} %bitcast.23, f32[128,256]{1,0:T(8,128)S(1)} %copy-done.3, f32[4096,256]{1,0:T(8,128)S(1)} %copy-done, s32[2560,1]{1,0:T(8,128)S(1)} %add.131.rem, s32[1,2560]{1,0:T(1,128)S(1)} %add.127.row, ...), custom_call_target="tpu_custom_call" | custom-call | tf_op jit(solution)/shard_map/reduce_update/pallas_call | solution.py:312
  101.8 2.7 %convert_subtract_fusion = f32[4096,256]{1,0:T(8,128)} fusion(f32[4096,256]{1,0:T(8,128)S(1)} %copy-done.1, bf16[32,128,256]{2,1,0:T(8,128)(2,1)S(1)} %get-tuple-element.14), kind=kLoop, calls=%fused_computation.12 | loop fusion | flops 2097152 | bytes 10485760 | tf_op jit(solution)/shard_map/sub | solution.py:414
  104.5 1.8 %divide_subtract_fusion = (f32[1024,256]{1,0:T(8,128)}, f32[1024,256]{1,0:T(8,128)}) fusion(f32[1024,256]{1,0:T(8,128)S(1)} %copy-done.7, f32[1024,256]{1,0:T(8,128)S(1)} %get-tuple-element.13, f32[1024,256]{1,0:T(8,128)S(1)} %copy-done.8), kind=kLoop, calls=%fused_computation.22 | loop fusion | flops 1572864 | bytes 5242880 | tf_op jit(solution)/shard_map/sub | solution.py:18
  106.3 0.7 copy.18
  (28 shorter events, 0.7 us)
Async XLA Ops:
  2.2 0.8 copy-start.4
  36.6 3.5 %copy-start.6 = (f32[1024,256]{1,0:T(8,128)S(1)}, f32[1024,256]{1,0:T(8,128)}, u32[]{:S(2)}) copy-start(f32[1024,256]{1,0:T(8,128)} %param.7) | copy-start | bytes 3145732
  44.9 9.5 %copy-start.5 = (f32[32,80,256]{2,1,0:T(8,128)S(1)}, f32[32,80,256]{2,1,0:T(8,128)}, u32[]{:S(2)}) copy-start(f32[32,80,256]{2,1,0:T(8,128)} %fusion.19) | copy-start | bytes 7864324
  54.4 0.9 copy-start.3
  55.3 2.2 %copy-start = (f32[4096,256]{1,0:T(8,128)S(1)}, f32[4096,256]{1,0:T(8,128)}, u32[]{:S(2)}) copy-start(f32[4096,256]{1,0:T(8,128)} %table.1) | copy-start | bytes 12582916
  57.5 1.6 %copy-start.2 = (bf16[16,256,256]{2,1,0:T(8,128)(2,1)S(1)}, bf16[16,256,256]{2,1,0:T(8,128)(2,1)}, u32[]{:S(2)}) copy-start(bf16[16,256,256]{2,1,0:T(8,128)(2,1)} %fusion.13) | copy-start | bytes 6291460
  59.1 42.7 %copy-start.1 = (f32[4096,256]{1,0:T(8,128)S(1)}, f32[4096,256]{1,0:T(8,128)}, u32[]{:S(2)}) copy-start(f32[4096,256]{1,0:T(8,128)} %table.1) | copy-start | bytes 12582916
  101.8 2.7 %copy-start.7 = (f32[1024,256]{1,0:T(8,128)S(1)}, f32[1024,256]{1,0:T(8,128)}, u32[]{:S(2)}) copy-start(f32[1024,256]{1,0:T(8,128)} %param.7) | copy-start | bytes 3145732
  101.8 2.7 %copy-start.8 = (f32[1024,256]{1,0:T(8,128)S(1)}, f32[1024,256]{1,0:T(8,128)}, u32[]{:S(2)}) copy-start(f32[1024,256]{1,0:T(8,128)} %param.8) | copy-start | bytes 3145732
